TPU v7x, 128 devices: a whole 4x4x4 slice. The times are simulated.
128 devices in a mesh: seq: 32 (over x, y, core), mp: 4 (over z).
Axes of the slice: x: 4, y: 4, z: 4, core: 2. Of those that a mesh axis runs over, the one named last changes fastest.
Arguments:
- values: bfloat16 [8192, 8192], P('seq', 'mp'), may hold values from -6 to 6
- k_first: bfloat16 [8192, 8192], P('seq', 'mp'), may hold values from -6 to 6
- q_first: bfloat16 [8192, 8192], P('seq', 'mp'), may hold values from -6 to 6
- k_second: bfloat16 [8192, 8192], P('seq', 'mp'), may hold values from -6 to 6
- q_second: bfloat16 [8192, 8192], P('seq', 'mp'), may hold values from -210 to 210
- mr_taps: bfloat16 [128, 8192], P(None, 'mp'), may hold values from -0.5 to 0.5
- li_rate: float32 [16, 8192], P(None, 'mp'), may hold values from 0 to 1, as said below
- li_residue: float32 [16, 8192], P(None, 'mp'), may hold values from -4 to 4
- tile_docs: int32 [64], replicated, may hold values from 0 to 7, never falling along the last dimension, each value on 1 to 32 neighbouring positions
Outputs:
- mixed: bfloat16 [8192, 8192], P('seq', 'mp')
Inputs may be any that keep to these rules, and one draw needn't show every extreme that they name: `tile_docs`: ids never fall along the sequence; a document spans at most 32 tiles. `li_rate`: positive decay rates.
All inputs are finite; a program needn't handle non-finite values.
Results may differ from a plain program's by a relative error of at most 0.012.
Values may be sent and summed in bfloat16 or wider, within the bound.
A program may use at most 320 MiB of HBM per device.

v0:
```python
import jax
import jax.numpy as jnp
import numpy as np
from jax import lax
from jax.sharding import PartitionSpec as P

TILE = 128
MR_TAPS = 128


norm_eps = 1e-06
top_precision = lax.Precision.HIGHEST
sub_rows = 32


def from_behind(value, axis, steps):
    count = lax.axis_size(axis)
    first, last = (max(0, -steps), min(count, count - steps))
    return lax.ppermute(value, axis, [(source, source + steps) for source in range(first, last)])


def band_index(offset, limit):
    later = np.arange(sub_rows)[:, None]
    earlier = np.arange(sub_rows)[None, :]
    lag_table = offset + later - earlier
    valid = (lag_table >= 0) & (lag_table < limit)
    return (np.where(valid, lag_table, 0), valid)


def banded(taps, index_table, valid):
    return jnp.where(valid[:, :, None], taps[index_table], jnp.zeros((), taps.dtype))


def run_tiles(start_state, tile_ends, kept, decay):

    def advance(carried, scan_item):
        tile_end, kept_flag = scan_item
        entered = carried * kept_flag
        return (decay * entered + tile_end, entered)

    return lax.scan(advance, start_state, (tile_ends, kept))


def on_device(
    values, k_first, q_first, k_second, q_second, mr_taps, li_rate, li_residue, tile_docs
):
    row_count, channels = values.shape
    tile_count = row_count // TILE
    sub_count = row_count // sub_rows
    per_tile = TILE // sub_rows
    first_tile = lax.axis_index("seq") * tile_count
    marked = jnp.concatenate([jnp.full((1,), -1, jnp.int32), tile_docs])
    doc_window = lax.dynamic_slice_in_dim(marked, first_tile, tile_count + 1)
    kept = (doc_window[1:] == doc_window[:-1]).astype(jnp.float32)
    through = (doc_window[tile_count] == doc_window[0]).astype(jnp.float32)
    position = jnp.arange(sub_count, dtype=jnp.int32) % per_tile
    kept_tile = jnp.repeat(kept, per_tile)
    kept_sub = jnp.where(position == 0, kept_tile, 1.0)
    gated_in = (k_first.astype(jnp.float32) * values.astype(jnp.float32)).astype(jnp.bfloat16)
    edge = from_behind(gated_in[row_count - (MR_TAPS - 1) :], "seq", 1)
    extended = jnp.concatenate([jnp.zeros((1, channels), jnp.bfloat16), edge, gated_in], axis=0)
    ext_tiles = extended.reshape(sub_count + per_tile, sub_rows, channels)
    shape_sub = (sub_count, sub_rows, channels)
    conv_out = jnp.zeros(shape_sub, jnp.float32)
    for lag_block in range(per_tile + 1):
        index_table, valid = band_index(lag_block * sub_rows, MR_TAPS)
        table = banded(mr_taps, index_table, valid)
        source = ext_tiles[per_tile - lag_block : per_tile - lag_block + sub_count]
        part_out = jnp.einsum("jic,nic->njc", table, source, preferred_element_type=jnp.float32)
        weight = jnp.where(position >= lag_block, 1.0, kept_tile)
        conv_out = conv_out + weight[:, None, None] * part_out
    short_out = (q_first.astype(jnp.float32).reshape(shape_sub) * conv_out).astype(jnp.bfloat16)
    long_in = (
        k_second.astype(jnp.float32).reshape(shape_sub) * short_out.astype(jnp.float32)
    ).astype(jnp.bfloat16)
    long_wide = long_in.astype(jnp.float32)
    lag_steps = jnp.arange(sub_rows, dtype=jnp.float32)
    amplitude = li_residue * jnp.sqrt(li_rate)
    end_weights = jnp.exp(-li_rate[:, None, :] * (sub_rows - 1 - lag_steps)[None, :, None])
    out_weights = amplitude[None] * jnp.exp(-li_rate[None] * (lag_steps + 1.0)[:, None, None])
    filter_taps = jnp.sum(
        amplitude[None] * jnp.exp(-li_rate[None] * lag_steps[:, None, None]), axis=1
    )
    decay = jnp.exp(-li_rate * sub_rows)
    inner_idx, inner_ok = band_index(0, sub_rows)
    inside_all = jnp.einsum(
        "jic,nic->njc", banded(filter_taps, inner_idx, inner_ok), long_wide, precision=top_precision
    )
    ends_all = jnp.einsum("mjc,njc->nmc", end_weights, long_wide, precision=top_precision)
    local_end, unused_entries = run_tiles(jnp.zeros_like(decay), ends_all, kept_sub, decay)
    block_decay = jnp.exp(-li_rate * row_count) * through

    def relay(step_no, incoming):
        return from_behind(block_decay * incoming + local_end, "seq", 1)

    arriving = lax.fori_loop(0, lax.axis_size("seq") - 1, relay, jnp.zeros_like(local_end))
    final_state, entering = run_tiles(arriving, ends_all, kept_sub, decay)
    state_part = jnp.einsum("jmc,nmc->njc", out_weights, entering, precision=top_precision)
    long_out = q_second.astype(jnp.float32).reshape(shape_sub) * (state_part + inside_all)
    long_out = long_out.reshape(row_count, channels)
    power = lax.psum(jnp.sum(long_out * long_out, axis=1), "mp")
    scale_rows = lax.rsqrt(power / (channels * lax.axis_size("mp")) + norm_eps)
    return (long_out * scale_rows[:, None]).astype(jnp.bfloat16)


def solution(mesh):
    return jax.shard_map(
        on_device,
        mesh=mesh,
        in_specs=(
            P("seq", "mp"),
            P("seq", "mp"),
            P("seq", "mp"),
            P("seq", "mp"),
            P("seq", "mp"),
            P(None, "mp"),
            P(None, "mp"),
            P(None, "mp"),
            P(),
        ),
        out_specs=P("seq", "mp"),
        check_vma=False,
    )
```

profile of v0, /device:TPU:2, one launch (start us, length us, event | category | flops | bytes accessed | tf_op | source)
XLA Modules:
  0.0 749.5 jit_solution(3701020155201919364)
XLA Ops:
  17.2 23.1 %copy.92 = bf16[32,32,2048]{1,0,2:T(8,128)(2,1)} copy(bf16[32,32,2048]{2,1,0:T(8,128)(2,1)} %bitcast.67) | data formatting | bytes 8388608 | tf_op jit(solution)/shard_map/gather | solution.py:31
  45.8 12.8 %multiply_reduce_fusion = f32[32,2048]{0,1:T(8,128)S(1)} fusion(f32[16,2048]{0,1:T(8,128)} %copy.104, f32[16,2048]{0,1:T(8,128)} %copy.107), kind=kLoop, calls=%fused_computation.15 | loop fusion | flops 3080192 | bytes 524288 | tf_op jit(solution)/shard_map/reduce_sum | solution.py:81
  58.6 15.0 %fusion.13 = f32[2048,8,32]{2,1,0:T(8,128)} fusion(bf16[8,32,2048]{1,0,2:T(8,128)(2,1)} %copy.93, bf16[32,32,2048]{1,0,2:T(8,128)(2,1)} %copy.92, pred[32,32]{1,0:T(8,128)(4,1)S(1)} %bitcast.80), kind=kOutput, calls=%fused_computation.25 | convolution fusion | flops 35651584 | bytes 7341056 | tf_op jit(solution)/shard_map/jic,nic->njc/dot_general | solution.py:69
  79.8 23.0 %copy.100 = bf16[32,32,2048]{1,0,2:T(8,128)(2,1)} copy(bf16[32,32,2048]{2,1,0:T(8,128)(2,1)} %bitcast.68) | data formatting | bytes 8388608 | tf_op jit(solution)/shard_map/gather | solution.py:31
  108.8 23.1 %copy.95 = bf16[32,32,2048]{1,0,2:T(8,128)(2,1)} copy(bf16[32,32,2048]{2,1,0:T(8,128)(2,1)} %bitcast.69) | data formatting | bytes 8388608 | tf_op jit(solution)/shard_map/gather | solution.py:31
  137.8 23.1 %copy.97 = bf16[32,32,2048]{1,0,2:T(8,128)(2,1)} copy(bf16[32,32,2048]{2,1,0:T(8,128)(2,1)} %bitcast.70) | data formatting | bytes 8388608 | tf_op jit(solution)/shard_map/gather | solution.py:31
  166.9 23.5 %copy.99 = bf16[32,32,2048]{1,0,2:T(8,128)(2,1)} copy(bf16[32,32,2048]{2,1,0:T(8,128)(2,1)} %bitcast.71) | data formatting | bytes 8388608 | tf_op jit(solution)/shard_map/gather | solution.py:31
  202.5 6.8 gather_fusion.5
  209.4 26.3 %copy.111 = f32[32,32,2048]{1,0,2:T(8,128)} copy(f32[32,32,2048]{2,1,0:T(8,128)} %bitcast.66) | data formatting | bytes 16777216 | tf_op jit(solution)/shard_map/gather | solution.py:31
  257.1 15.0 %fusion.36 = f32[2048,8,32]{2,1,0:T(8,128)} fusion(bf16[8,32,2048]{1,0,2:T(8,128)(2,1)} %copy.94, bf16[32,32,2048]{1,0,2:T(8,128)(2,1)} %copy.95), kind=kOutput, calls=%fused_computation.80 | convolution fusion | flops 33554432 | bytes 7340032 | tf_op jit(solution)/shard_map/jic,nic->njc/dot_general | solution.py:69
  272.1 14.2 %fusion.37 = f32[2048,8,32]{2,1,0:T(8,128)} fusion(bf16[8,32,2048]{1,0,2:T(8,128)(2,1)S(1)} %copy-done.3, bf16[32,32,2048]{1,0,2:T(8,128)(2,1)} %copy.97), kind=kOutput, calls=%fused_computation.81 | convolution fusion | flops 33554432 | bytes 7340032 | tf_op jit(solution)/shard_map/jic,nic->njc/dot_general | solution.py:69
  286.3 15.0 %fusion.11 = f32[2048,8,32]{2,1,0:T(8,128)} fusion(bf16[8,32,2048]{1,0,2:T(8,128)(2,1)} %copy.101, bf16[32,32,2048]{1,0,2:T(8,128)(2,1)} %copy.100, pred[32,32]{1,0:T(8,128)(4,1)S(1)} %bitcast.82), kind=kOutput, calls=%fused_computation.23 | convolution fusion | flops 35651584 | bytes 7341056 | tf_op jit(solution)/shard_map/jic,nic->njc/dot_general | solution.py:69
  301.3 23.9 %multiply_convert_fusion = bf16[8,32,2048]{1,0,2:T(8,128)(2,1)S(1)} fusion(f32[8,32,2048]{1,0,2:T(8,128)} %copy.103, f32[8,32,2048]{1,0,2:T(8,128)} %copy.102, f32[2048,8,32]{2,1,0:T(8,128)} %fusion.11, f32[2048,8,32]{2,1,0:T(8,128)} %fusion.37, f32[2048,8,32]{2,1,0:T(8,128)} %fusion.36, f32[2048,8,32]{2,1,0:T(8,128)} %fusion.13, ...), kind=kOutput, calls=%fused_computation.37 | convolution fusion | flops 40894464 | bytes 18874528 | tf_op jit(solution)/shard_map/jic,nic->njc/dot_general | solution.py:69
  327.2 30.8 %fusion.1 = f32[2048,8,32]{2,1,0:T(8,128)} fusion(bf16[8,32,2048]{1,0,2:T(8,128)(2,1)S(1)} %multiply_convert_fusion, f32[32,32,2048]{1,0,2:T(8,128)} %copy.111, pred[32,32]{1,0:T(8,128)(4,1)S(1)} %bitcast.81), kind=kOutput, calls=%fused_computation.12 | convolution fusion | flops 203423744 | bytes 11535360 | tf_op jit(solution)/shard_map/jic,nic->njc/dot_general | solution.py:86
  363.1 18.6 %fusion.26 = f32[8,16,2048]{1,0,2:T(8,128)} fusion(bf16[8,32,2048]{1,0,2:T(8,128)(2,1)} %copy-done.2, f32[32]{0:T(128)S(1)} %iota_subtract_fusion, f32[16,2048]{0,1:T(8,128)} %copy.104), kind=kOutput, calls=%fused_computation.40 | convolution fusion | flops 101711872 | bytes 2228352 | tf_op jit(solution)/shard_map/mjc,njc->nmc/dot_general | solution.py:89
  387.8 17.1 %while.35 = (s32[]{:T(128)}, f32[16,2048]{1,0:T(8,128)S(1)}, f32[8]{0:T(128)S(1)}, f32[16,2048]{1,0:T(8,128)S(1)}, f32[8,16,2048]{2,1,0:T(8,128)}, /*index=5*/s32[]{:T(128)}, s32[]{:T(128)}) while((s32[]{:T(128)}, f32[16,2048]{1,0:T(8,128)S(1)}, f32[8]{0:T(128)S(1)}, f32[16,2048]{1,0:T(8,128)S(1)}, f32[8,16,2048]{2,1,0:T(8,128)}, ...), condition=%wide.region_1.2_spmd.clone, body=%wide.region_0.1_spmd.clone.sunk | while | flops 131075 | bytes 524395 | solution.py:41
  404.9 261.1 %while.33 = (s32[]{:T(128)}, f32[16,2048]{1,0:T(8,128)S(1)}, f32[16,2048]{1,0:T(8,128)S(1)}, f32[16,2048]{1,0:T(8,128)S(1)}, s32[]{:T(128)}) while((s32[]{:T(128)}, f32[16,2048]{1,0:T(8,128)S(1)}, f32[16,2048]{1,0:T(8,128)S(1)}, f32[16,2048]{1,0:T(8,128)S(1)}, s32[]{:T(128)}) %tuple.83), condition=%wide.region_3.4_spmd, body=%wide.region_2.3_spmd.sunk | while | flops 65538 | bytes 1048677 | solution.py:96
  415.3 6.5 collective-permute-done
  440.6 6.5 collective-permute-done
  449.0 6.5 collective-permute-done
  474.3 6.5 collective-permute-done
  482.7 6.5 collective-permute-done
  508.0 6.5 collective-permute-done
  516.4 6.5 collective-permute-done
  533.2 6.5 collective-permute-done
  541.7 6.5 collective-permute-done
  566.9 6.5 collective-permute-done
  575.3 6.5 collective-permute-done
  600.6 6.5 collective-permute-done
  666.0 27.9 %while.34 = (s32[]{:T(128)}, f32[16,2048]{1,0:T(8,128)S(1)}, f32[8,16,2048]{2,1,0:T(8,128)}, f32[8]{0:T(128)S(1)}, f32[16,2048]{1,0:T(8,128)S(1)}, /*index=5*/f32[8,16,2048]{2,1,0:T(8,128)}, s32[]{:T(128)}) while((s32[]{:T(128)}, f32[16,2048]{1,0:T(8,128)S(1)}, f32[8,16,2048]{2,1,0:T(8,128)}, f32[8]{0:T(128)S(1)}, f32[16,2048]{1,0:T(8,128)S(1)}, ...), condition=%wide.region_5.6_spmd, body=%wide.region_4.5_spmd.sunk | while | flops 131074 | bytes 787553 | solution.py:41
  700.0 24.9 %fusion.4 = f32[2048,8,32]{2,1,0:T(8,128)} fusion(f32[8,16,2048]{1,0,2:T(8,128)} %copy.109, f32[32]{0:T(128)S(1)} %iota_add_fusion, f32[16,2048]{0,1:T(8,128)} %copy.104, f32[16,2048]{0,1:T(8,128)} %copy.107), kind=kOutput, calls=%fused_computation.16 | convolution fusion | flops 102760448 | bytes 3408000 | tf_op jit(solution)/shard_map/jmc,nmc->njc/dot_general | solution.py:98
  734.7 11.7 %psum.7 = f32[256]{0:T(256)S(1)} all-reduce(f32[256]{0:T(256)S(1)} %reduce_sum.22), channel_id=1, replica_groups=mesh['seq'=32,'mp'=4] {'mp'}, use_global_device_ids=true, to_apply=%region_8.9 | all-reduce | flops 256 | bytes 2048 | tf_op jit(solution)/shard_map/psum | solution.py:101
  (204 shorter events, 338.8 us)
Async XLA Ops:
  2.9 232.8 %collective-permute-start.1 = (bf16[127,2048]{1,0:T(8,128)(2,1)}, bf16[127,2048]{1,0:T(8,128)(2,1)S(1)}, u32[]{:S(2)}, u32[]{:S(2)}) collective-permute-start(bf16[127,2048]{1,0:T(8,128)(2,1)} %slice.72), channel_id=1, source_target_pairs={{0,4},{4,8},{8,12},{12,16},{16,20},{20,24},{24,28},{28,32},{32,36}... | collective-permute-start | bytes 1560584 | tf_op jit(solution)/shard_map/ppermute | solution.py:19
  405.0 8.4 %collective-permute-start = (f32[16,2048]{1,0:T(8,128)S(1)}, f32[16,2048]{1,0:T(8,128)S(1)}, u32[]{:S(2)}, u32[]{:S(2)}) collective-permute-start(f32[16,2048]{1,0:T(8,128)S(1)} %multiply_add_fusion.2), channel_id=1, source_target_pairs={{0,4},{4,8},{8,12},{12,16},{16,20},{20,24},{24,28},{28,32},{32,36}... | collective-permute-start | bytes 393224 | tf_op jit(solution)/shard_map/while/body/eval_jaxpr/ppermute | solution.py:19
  413.4 8.4 %collective-permute-start = (f32[16,2048]{1,0:T(8,128)S(1)}, f32[16,2048]{1,0:T(8,128)S(1)}, u32[]{:S(2)}, u32[]{:S(2)}) collective-permute-start(f32[16,2048]{1,0:T(8,128)S(1)} %multiply_add_fusion.2), channel_id=1, source_target_pairs={{0,4},{4,8},{8,12},{12,16},{16,20},{20,24},{24,28},{28,32},{32,36}... | collective-permute-start | bytes 393224 | tf_op jit(solution)/shard_map/while/body/eval_jaxpr/ppermute | solution.py:19
  421.8 8.4 %collective-permute-start = (f32[16,2048]{1,0:T(8,128)S(1)}, f32[16,2048]{1,0:T(8,128)S(1)}, u32[]{:S(2)}, u32[]{:S(2)}) collective-permute-start(f32[16,2048]{1,0:T(8,128)S(1)} %multiply_add_fusion.2), channel_id=1, source_target_pairs={{0,4},{4,8},{8,12},{12,16},{16,20},{20,24},{24,28},{28,32},{32,36}... | collective-permute-start | bytes 393224 | tf_op jit(solution)/shard_map/while/body/eval_jaxpr/ppermute | solution.py:19
  430.2 8.4 %collective-permute-start = (f32[16,2048]{1,0:T(8,128)S(1)}, f32[16,2048]{1,0:T(8,128)S(1)}, u32[]{:S(2)}, u32[]{:S(2)}) collective-permute-start(f32[16,2048]{1,0:T(8,128)S(1)} %multiply_add_fusion.2), channel_id=1, source_target_pairs={{0,4},{4,8},{8,12},{12,16},{16,20},{20,24},{24,28},{28,32},{32,36}... | collective-permute-start | bytes 393224 | tf_op jit(solution)/shard_map/while/body/eval_jaxpr/ppermute | solution.py:19
  438.7 8.4 %collective-permute-start = (f32[16,2048]{1,0:T(8,128)S(1)}, f32[16,2048]{1,0:T(8,128)S(1)}, u32[]{:S(2)}, u32[]{:S(2)}) collective-permute-start(f32[16,2048]{1,0:T(8,128)S(1)} %multiply_add_fusion.2), channel_id=1, source_target_pairs={{0,4},{4,8},{8,12},{12,16},{16,20},{20,24},{24,28},{28,32},{32,36}... | collective-permute-start | bytes 393224 | tf_op jit(solution)/shard_map/while/body/eval_jaxpr/ppermute | solution.py:19
  447.1 8.4 %collective-permute-start = (f32[16,2048]{1,0:T(8,128)S(1)}, f32[16,2048]{1,0:T(8,128)S(1)}, u32[]{:S(2)}, u32[]{:S(2)}) collective-permute-start(f32[16,2048]{1,0:T(8,128)S(1)} %multiply_add_fusion.2), channel_id=1, source_target_pairs={{0,4},{4,8},{8,12},{12,16},{16,20},{20,24},{24,28},{28,32},{32,36}... | collective-permute-start | bytes 393224 | tf_op jit(solution)/shard_map/while/body/eval_jaxpr/ppermute | solution.py:19
  455.5 8.4 %collective-permute-start = (f32[16,2048]{1,0:T(8,128)S(1)}, f32[16,2048]{1,0:T(8,128)S(1)}, u32[]{:S(2)}, u32[]{:S(2)}) collective-permute-start(f32[16,2048]{1,0:T(8,128)S(1)} %multiply_add_fusion.2), channel_id=1, source_target_pairs={{0,4},{4,8},{8,12},{12,16},{16,20},{20,24},{24,28},{28,32},{32,36}... | collective-permute-start | bytes 393224 | tf_op jit(solution)/shard_map/while/body/eval_jaxpr/ppermute | solution.py:19
  463.9 8.4 %collective-permute-start = (f32[16,2048]{1,0:T(8,128)S(1)}, f32[16,2048]{1,0:T(8,128)S(1)}, u32[]{:S(2)}, u32[]{:S(2)}) collective-permute-start(f32[16,2048]{1,0:T(8,128)S(1)} %multiply_add_fusion.2), channel_id=1, source_target_pairs={{0,4},{4,8},{8,12},{12,16},{16,20},{20,24},{24,28},{28,32},{32,36}... | collective-permute-start | bytes 393224 | tf_op jit(solution)/shard_map/while/body/eval_jaxpr/ppermute | solution.py:19
  472.3 8.4 %collective-permute-start = (f32[16,2048]{1,0:T(8,128)S(1)}, f32[16,2048]{1,0:T(8,128)S(1)}, u32[]{:S(2)}, u32[]{:S(2)}) collective-permute-start(f32[16,2048]{1,0:T(8,128)S(1)} %multiply_add_fusion.2), channel_id=1, source_target_pairs={{0,4},{4,8},{8,12},{12,16},{16,20},{20,24},{24,28},{28,32},{32,36}... | collective-permute-start | bytes 393224 | tf_op jit(solution)/shard_map/while/body/eval_jaxpr/ppermute | solution.py:19
  480.8 8.4 %collective-permute-start = (f32[16,2048]{1,0:T(8,128)S(1)}, f32[16,2048]{1,0:T(8,128)S(1)}, u32[]{:S(2)}, u32[]{:S(2)}) collective-permute-start(f32[16,2048]{1,0:T(8,128)S(1)} %multiply_add_fusion.2), channel_id=1, source_target_pairs={{0,4},{4,8},{8,12},{12,16},{16,20},{20,24},{24,28},{28,32},{32,36}... | collective-permute-start | bytes 393224 | tf_op jit(solution)/shard_map/while/body/eval_jaxpr/ppermute | solution.py:19
  489.2 8.4 %collective-permute-start = (f32[16,2048]{1,0:T(8,128)S(1)}, f32[16,2048]{1,0:T(8,128)S(1)}, u32[]{:S(2)}, u32[]{:S(2)}) collective-permute-start(f32[16,2048]{1,0:T(8,128)S(1)} %multiply_add_fusion.2), channel_id=1, source_target_pairs={{0,4},{4,8},{8,12},{12,16},{16,20},{20,24},{24,28},{28,32},{32,36}... | collective-permute-start | bytes 393224 | tf_op jit(solution)/shard_map/while/body/eval_jaxpr/ppermute | solution.py:19
  497.6 8.4 %collective-permute-start = (f32[16,2048]{1,0:T(8,128)S(1)}, f32[16,2048]{1,0:T(8,128)S(1)}, u32[]{:S(2)}, u32[]{:S(2)}) collective-permute-start(f32[16,2048]{1,0:T(8,128)S(1)} %multiply_add_fusion.2), channel_id=1, source_target_pairs={{0,4},{4,8},{8,12},{12,16},{16,20},{20,24},{24,28},{28,32},{32,36}... | collective-permute-start | bytes 393224 | tf_op jit(solution)/shard_map/while/body/eval_jaxpr/ppermute | solution.py:19
  506.0 8.4 %collective-permute-start = (f32[16,2048]{1,0:T(8,128)S(1)}, f32[16,2048]{1,0:T(8,128)S(1)}, u32[]{:S(2)}, u32[]{:S(2)}) collective-permute-start(f32[16,2048]{1,0:T(8,128)S(1)} %multiply_add_fusion.2), channel_id=1, source_target_pairs={{0,4},{4,8},{8,12},{12,16},{16,20},{20,24},{24,28},{28,32},{32,36}... | collective-permute-start | bytes 393224 | tf_op jit(solution)/shard_map/while/body/eval_jaxpr/ppermute | solution.py:19
  514.5 8.4 %collective-permute-start = (f32[16,2048]{1,0:T(8,128)S(1)}, f32[16,2048]{1,0:T(8,128)S(1)}, u32[]{:S(2)}, u32[]{:S(2)}) collective-permute-start(f32[16,2048]{1,0:T(8,128)S(1)} %multiply_add_fusion.2), channel_id=1, source_target_pairs={{0,4},{4,8},{8,12},{12,16},{16,20},{20,24},{24,28},{28,32},{32,36}... | collective-permute-start | bytes 393224 | tf_op jit(solution)/shard_map/while/body/eval_jaxpr/ppermute | solution.py:19
  522.9 8.4 %collective-permute-start = (f32[16,2048]{1,0:T(8,128)S(1)}, f32[16,2048]{1,0:T(8,128)S(1)}, u32[]{:S(2)}, u32[]{:S(2)}) collective-permute-start(f32[16,2048]{1,0:T(8,128)S(1)} %multiply_add_fusion.2), channel_id=1, source_target_pairs={{0,4},{4,8},{8,12},{12,16},{16,20},{20,24},{24,28},{28,32},{32,36}... | collective-permute-start | bytes 393224 | tf_op jit(solution)/shard_map/while/body/eval_jaxpr/ppermute | solution.py:19
  531.3 8.4 %collective-permute-start = (f32[16,2048]{1,0:T(8,128)S(1)}, f32[16,2048]{1,0:T(8,128)S(1)}, u32[]{:S(2)}, u32[]{:S(2)}) collective-permute-start(f32[16,2048]{1,0:T(8,128)S(1)} %multiply_add_fusion.2), channel_id=1, source_target_pairs={{0,4},{4,8},{8,12},{12,16},{16,20},{20,24},{24,28},{28,32},{32,36}... | collective-permute-start | bytes 393224 | tf_op jit(solution)/shard_map/while/body/eval_jaxpr/ppermute | solution.py:19
  539.7 8.4 %collective-permute-start = (f32[16,2048]{1,0:T(8,128)S(1)}, f32[16,2048]{1,0:T(8,128)S(1)}, u32[]{:S(2)}, u32[]{:S(2)}) collective-permute-start(f32[16,2048]{1,0:T(8,128)S(1)} %multiply_add_fusion.2), channel_id=1, source_target_pairs={{0,4},{4,8},{8,12},{12,16},{16,20},{20,24},{24,28},{28,32},{32,36}... | collective-permute-start | bytes 393224 | tf_op jit(solution)/shard_map/while/body/eval_jaxpr/ppermute | solution.py:19
  548.1 8.4 %collective-permute-start = (f32[16,2048]{1,0:T(8,128)S(1)}, f32[16,2048]{1,0:T(8,128)S(1)}, u32[]{:S(2)}, u32[]{:S(2)}) collective-permute-start(f32[16,2048]{1,0:T(8,128)S(1)} %multiply_add_fusion.2), channel_id=1, source_target_pairs={{0,4},{4,8},{8,12},{12,16},{16,20},{20,24},{24,28},{28,32},{32,36}... | collective-permute-start | bytes 393224 | tf_op jit(solution)/shard_map/while/body/eval_jaxpr/ppermute | solution.py:19
  556.6 8.4 %collective-permute-start = (f32[16,2048]{1,0:T(8,128)S(1)}, f32[16,2048]{1,0:T(8,128)S(1)}, u32[]{:S(2)}, u32[]{:S(2)}) collective-permute-start(f32[16,2048]{1,0:T(8,128)S(1)} %multiply_add_fusion.2), channel_id=1, source_target_pairs={{0,4},{4,8},{8,12},{12,16},{16,20},{20,24},{24,28},{28,32},{32,36}... | collective-permute-start | bytes 393224 | tf_op jit(solution)/shard_map/while/body/eval_jaxpr/ppermute | solution.py:19
  565.0 8.4 %collective-permute-start = (f32[16,2048]{1,0:T(8,128)S(1)}, f32[16,2048]{1,0:T(8,128)S(1)}, u32[]{:S(2)}, u32[]{:S(2)}) collective-permute-start(f32[16,2048]{1,0:T(8,128)S(1)} %multiply_add_fusion.2), channel_id=1, source_target_pairs={{0,4},{4,8},{8,12},{12,16},{16,20},{20,24},{24,28},{28,32},{32,36}... | collective-permute-start | bytes 393224 | tf_op jit(solution)/shard_map/while/body/eval_jaxpr/ppermute | solution.py:19
  573.4 8.4 %collective-permute-start = (f32[16,2048]{1,0:T(8,128)S(1)}, f32[16,2048]{1,0:T(8,128)S(1)}, u32[]{:S(2)}, u32[]{:S(2)}) collective-permute-start(f32[16,2048]{1,0:T(8,128)S(1)} %multiply_add_fusion.2), channel_id=1, source_target_pairs={{0,4},{4,8},{8,12},{12,16},{16,20},{20,24},{24,28},{28,32},{32,36}... | collective-permute-start | bytes 393224 | tf_op jit(solution)/shard_map/while/body/eval_jaxpr/ppermute | solution.py:19
  581.8 8.4 %collective-permute-start = (f32[16,2048]{1,0:T(8,128)S(1)}, f32[16,2048]{1,0:T(8,128)S(1)}, u32[]{:S(2)}, u32[]{:S(2)}) collective-permute-start(f32[16,2048]{1,0:T(8,128)S(1)} %multiply_add_fusion.2), channel_id=1, source_target_pairs={{0,4},{4,8},{8,12},{12,16},{16,20},{20,24},{24,28},{28,32},{32,36}... | collective-permute-start | bytes 393224 | tf_op jit(solution)/shard_map/while/body/eval_jaxpr/ppermute | solution.py:19
  590.3 8.4 %collective-permute-start = (f32[16,2048]{1,0:T(8,128)S(1)}, f32[16,2048]{1,0:T(8,128)S(1)}, u32[]{:S(2)}, u32[]{:S(2)}) collective-permute-start(f32[16,2048]{1,0:T(8,128)S(1)} %multiply_add_fusion.2), channel_id=1, source_target_pairs={{0,4},{4,8},{8,12},{12,16},{16,20},{20,24},{24,28},{28,32},{32,36}... | collective-permute-start | bytes 393224 | tf_op jit(solution)/shard_map/while/body/eval_jaxpr/ppermute | solution.py:19
  598.7 8.4 %collective-permute-start = (f32[16,2048]{1,0:T(8,128)S(1)}, f32[16,2048]{1,0:T(8,128)S(1)}, u32[]{:S(2)}, u32[]{:S(2)}) collective-permute-start(f32[16,2048]{1,0:T(8,128)S(1)} %multiply_add_fusion.2), channel_id=1, source_target_pairs={{0,4},{4,8},{8,12},{12,16},{16,20},{20,24},{24,28},{28,32},{32,36}... | collective-permute-start | bytes 393224 | tf_op jit(solution)/shard_map/while/body/eval_jaxpr/ppermute | solution.py:19
  607.1 8.4 %collective-permute-start = (f32[16,2048]{1,0:T(8,128)S(1)}, f32[16,2048]{1,0:T(8,128)S(1)}, u32[]{:S(2)}, u32[]{:S(2)}) collective-permute-start(f32[16,2048]{1,0:T(8,128)S(1)} %multiply_add_fusion.2), channel_id=1, source_target_pairs={{0,4},{4,8},{8,12},{12,16},{16,20},{20,24},{24,28},{28,32},{32,36}... | collective-permute-start | bytes 393224 | tf_op jit(solution)/shard_map/while/body/eval_jaxpr/ppermute | solution.py:19
  615.5 8.4 %collective-permute-start = (f32[16,2048]{1,0:T(8,128)S(1)}, f32[16,2048]{1,0:T(8,128)S(1)}, u32[]{:S(2)}, u32[]{:S(2)}) collective-permute-start(f32[16,2048]{1,0:T(8,128)S(1)} %multiply_add_fusion.2), channel_id=1, source_target_pairs={{0,4},{4,8},{8,12},{12,16},{16,20},{20,24},{24,28},{28,32},{32,36}... | collective-permute-start | bytes 393224 | tf_op jit(solution)/shard_map/while/body/eval_jaxpr/ppermute | solution.py:19
  623.9 8.4 %collective-permute-start = (f32[16,2048]{1,0:T(8,128)S(1)}, f32[16,2048]{1,0:T(8,128)S(1)}, u32[]{:S(2)}, u32[]{:S(2)}) collective-permute-start(f32[16,2048]{1,0:T(8,128)S(1)} %multiply_add_fusion.2), channel_id=1, source_target_pairs={{0,4},{4,8},{8,12},{12,16},{16,20},{20,24},{24,28},{28,32},{32,36}... | collective-permute-start | bytes 393224 | tf_op jit(solution)/shard_map/while/body/eval_jaxpr/ppermute | solution.py:19
  632.4 8.4 %collective-permute-start = (f32[16,2048]{1,0:T(8,128)S(1)}, f32[16,2048]{1,0:T(8,128)S(1)}, u32[]{:S(2)}, u32[]{:S(2)}) collective-permute-start(f32[16,2048]{1,0:T(8,128)S(1)} %multiply_add_fusion.2), channel_id=1, source_target_pairs={{0,4},{4,8},{8,12},{12,16},{16,20},{20,24},{24,28},{28,32},{32,36}... | collective-permute-start | bytes 393224 | tf_op jit(solution)/shard_map/while/body/eval_jaxpr/ppermute | solution.py:19
  640.8 8.4 %collective-permute-start = (f32[16,2048]{1,0:T(8,128)S(1)}, f32[16,2048]{1,0:T(8,128)S(1)}, u32[]{:S(2)}, u32[]{:S(2)}) collective-permute-start(f32[16,2048]{1,0:T(8,128)S(1)} %multiply_add_fusion.2), channel_id=1, source_target_pairs={{0,4},{4,8},{8,12},{12,16},{16,20},{20,24},{24,28},{28,32},{32,36}... | collective-permute-start | bytes 393224 | tf_op jit(solution)/shard_map/while/body/eval_jaxpr/ppermute | solution.py:19
  649.2 8.4 %collective-permute-start = (f32[16,2048]{1,0:T(8,128)S(1)}, f32[16,2048]{1,0:T(8,128)S(1)}, u32[]{:S(2)}, u32[]{:S(2)}) collective-permute-start(f32[16,2048]{1,0:T(8,128)S(1)} %multiply_add_fusion.2), channel_id=1, source_target_pairs={{0,4},{4,8},{8,12},{12,16},{16,20},{20,24},{24,28},{28,32},{32,36}... | collective-permute-start | bytes 393224 | tf_op jit(solution)/shard_map/while/body/eval_jaxpr/ppermute | solution.py:19
  657.6 8.4 %collective-permute-start = (f32[16,2048]{1,0:T(8,128)S(1)}, f32[16,2048]{1,0:T(8,128)S(1)}, u32[]{:S(2)}, u32[]{:S(2)}) collective-permute-start(f32[16,2048]{1,0:T(8,128)S(1)} %multiply_add_fusion.2), channel_id=1, source_target_pairs={{0,4},{4,8},{8,12},{12,16},{16,20},{20,24},{24,28},{28,32},{32,36}... | collective-permute-start | bytes 393224 | tf_op jit(solution)/shard_map/while/body/eval_jaxpr/ppermute | solution.py:19
  (18 other events, 345.1 us)
where the time goes:
time: 761 us; the launch traced here: 749 us
  local copies, waits for them, and re-layouts  254 us (33%)
  waiting for transfers between devices  199 us (26%)
  matrix products  157 us (21%)
  starting transfers between devices  63.1 us (8%)
  other arithmetic  62.2 us (8%)
  blocking collectives  11.7 us (2%)
    ppermute x32, waiting for transfers between devices, from_behind(): lax.ppermute(value, axis, [(source, source + steps) for source in range(f...  199 us
    gather x12, local copies, waits for them, and re-layouts, banded(): taps[index_table]  179 us
    dot_general x5, matrix products, on_device(): jnp.einsum('jic,nic->njc', table, source, preferred_element_type=jnp.floa...  83.1 us
    ppermute x32, starting transfers between devices, from_behind(): lax.ppermute(value, axis, [(source, source + steps) for source in range(f...  63.1 us
    dot_general x1, matrix products, on_device(): jnp.einsum('jic,nic->njc', banded(filter_taps, inner_idx, inner_ok), long...  30.8 us
    add x16, other arithmetic, advance(): return (decay * entered + tile_end, entered)  25.3 us
    dot_general x1, matrix products, on_device(): jnp.einsum('jmc,nmc->njc', out_weights, entering, precision=top_precision)  24.9 us
    slice x7, local copies, waits for them, and re-layouts, on_device(): source = ext_tiles[per_tile - lag_block:per_tile - lag_block + sub_count]  23.6 us
  transfers between devices with their start and end apart: 32, of which 31 were waited for; matrix products, arithmetic and copies ran while one was open for 31% of the time, Pallas kernels for 0%

commit v1 on v0

v1 whole, which is shorter than its diff:
```python
import functools
import jax
import jax.numpy as jnp
import numpy as np
from jax import lax
from jax.experimental import pallas as pl
from jax.experimental.pallas import tpu as pltpu
from jax.sharding import PartitionSpec as P

TILE = 128
MODES = 16
LANES = 128
WIDE = 256
norm_eps = 1e-06
MESH = pl.DeviceIdType.MESH


def split_bf16(table):
    high = table.astype(jnp.bfloat16)
    low = (table - high.astype(np.float64)).astype(jnp.bfloat16)
    return np.asarray(high), np.asarray(low)


def dft_tables():
    freq = 2.0 * np.pi * (4.0 * np.arange(TILE) + 1.0) / (4.0 * TILE)
    angle = freq[:, None] * np.arange(TILE)[None, :]
    forward = np.concatenate([np.cos(angle), -np.sin(angle)], axis=0)
    inverse = forward.T / TILE
    f_high, f_low = split_bf16(forward)
    g_high, g_low = split_bf16(inverse)
    ahead = np.concatenate([f_high, f_low, f_high], axis=1)
    back = np.concatenate([g_high, g_low, g_high], axis=1)
    return ahead, back


def wait_bytes(ref, sem):
    pltpu.make_async_copy(ref, ref, sem).wait()


def kernel(
    seq_count, mp_count,
    docs, values_h, k1_h, q1_h, k2_h, q2_h, taps_h, rate_h, resid_h, ahead_h, back_h,
    out_h,
    values, k1, q1, k2, q2, taps, rate, resid, ahead, back,
    gated, halo, longin, inside, longout, amp, z8, z128, zb,
    acc1, ends0, esend, erecv, ssend, srecv, power, psend, precv, outbuf,
    in_sem, par_sem, halo_send, halo_recv, e_send, e_recv, s_send, s_recv, p_send, p_recv, out_sem,
):
    me = lax.axis_index("seq")
    part = lax.axis_index("mp")
    chunks = values.shape[1] // WIDE
    channels = values.shape[1]

    def in_copy(source, target, row, ch):
        cols = pl.ds(ch * WIDE, WIDE)
        return pltpu.make_async_copy(source.at[:, cols], target.at[:, cols], in_sem.at[row, ch])

    for ch in range(chunks):
        in_copy(values_h, values, 0, ch).start()
        in_copy(k1_h, k1, 1, ch).start()
    whole = [(rate_h, rate), (resid_h, resid), (taps_h, taps), (ahead_h, ahead), (back_h, back),
             (q1_h, q1), (k2_h, k2), (q2_h, q2)]
    whole_copies = [pltpu.make_async_copy(a, b, par_sem.at[n]) for n, (a, b) in enumerate(whole)]
    for copy in whole_copies:
        copy.start()

    barrier = pltpu.get_barrier_semaphore()

    def greet(step, carry):
        pl.semaphore_signal(barrier, inc=1, device_id=(lax.rem(me + step, seq_count), part), device_id_type=MESH)
        return carry

    lax.fori_loop(1, seq_count, greet, 0)
    for step in range(1, mp_count):
        pl.semaphore_signal(barrier, inc=1, device_id=(me, lax.rem(part + step, mp_count)), device_id_type=MESH)

    for ch in range(chunks):
        in_copy(values_h, values, 0, ch).wait()
        in_copy(k1_h, k1, 1, ch).wait()
        cols = pl.ds(ch * WIDE, WIDE)
        for half in (1, 0):
            rows = pl.ds(half * TILE, TILE)
            product = k1[rows, cols].astype(jnp.float32) * values[rows, cols].astype(jnp.float32)
            gated[half, ch] = product.astype(jnp.bfloat16)

    for copy in whole_copies[:2]:
        copy.wait()
    r_all = rate[...]
    amp[...] = resid[...] * jnp.sqrt(r_all)
    z8[...] = jnp.exp(-8.0 * r_all)
    z128[...] = jnp.exp(-float(TILE) * r_all)
    sub = lax.broadcasted_iota(jnp.int32, (8, LANES), 0).astype(jnp.float32)

    def fill_zb(group, carry):
        cols = pl.ds(pl.multiple_of(group * LANES, LANES), LANES)
        for m in range(MODES):
            zb[m, :, cols] = jnp.exp(-rate[m : m + 1, cols] * sub)
        return carry

    lax.fori_loop(0, channels // LANES, fill_zb, 0)

    pl.semaphore_wait(barrier, seq_count - 1 + mp_count - 1)
    after = lax.rem(me + 1, seq_count)

    def halo_copy(ch):
        return pltpu.make_async_remote_copy(
            src_ref=gated.at[1, ch], dst_ref=halo.at[ch], send_sem=halo_send, recv_sem=halo_recv.at[ch],
            device_id=(after, part), device_id_type=MESH)

    for ch in range(chunks):
        halo_copy(ch).start()

    first = 2 * me
    doc_before = docs[jnp.maximum(first - 1, 0)]
    doc_a = docs[first]
    doc_b = docs[first + 1]
    kept0 = jnp.where(jnp.logical_and(me > 0, doc_before == doc_a), 1.0, 0.0).astype(jnp.float32)
    kept1 = jnp.where(doc_a == doc_b, 1.0, 0.0).astype(jnp.float32)

    for copy in whole_copies[2:]:
        copy.wait()

    def transform(tile):
        doubled = jnp.concatenate([tile, tile], axis=0)
        return jnp.dot(ahead[:, : 2 * TILE], doubled, preferred_element_type=jnp.float32)

    def untransform(real, imag):
        real_high = real.astype(jnp.bfloat16)
        imag_high = imag.astype(jnp.bfloat16)
        real_low = (real - real_high.astype(jnp.float32)).astype(jnp.bfloat16)
        imag_low = (imag - imag_high.astype(jnp.float32)).astype(jnp.bfloat16)
        stacked = jnp.concatenate([real_high, imag_high, real_high, imag_high, real_low, imag_low], axis=0)
        return jnp.dot(back[...], stacked, preferred_element_type=jnp.float32)

    def short_tile(current, previous, kept, spectrum, rows, cols):
        real = current[:TILE] - kept * previous[TILE:]
        imag = current[TILE:] + kept * previous[:TILE]
        s_real, s_imag = spectrum[:TILE], spectrum[TILE:]
        conv = untransform(real * s_real - imag * s_imag, real * s_imag + imag * s_real)
        short = (q1[rows, cols].astype(jnp.float32) * conv).astype(jnp.bfloat16)
        return (k2[rows, cols].astype(jnp.float32) * short.astype(jnp.float32)).astype(jnp.bfloat16)

    def horner(tile, base):
        steps = [z8[m : m + 1, pl.ds(base, LANES)] for m in range(MODES)]
        sums = [tile[0:8]] * MODES
        for block in range(1, TILE // 8):
            row = tile[8 * block : 8 * block + 8]
            sums = [s * z + row for s, z in zip(sums, steps)]
        return sums

    def forward_chunk(ch, carry):
        start = pl.multiple_of(ch * WIDE, WIDE)
        cols = pl.ds(start, WIDE)
        spec0 = transform(gated[0, ch])
        spec1 = transform(gated[1, ch])
        spectrum = transform(taps[:, cols])
        late = short_tile(spec1, spec0, kept1, spectrum, pl.ds(TILE, TILE), cols)
        longin[1, ch] = late
        for group in range(2):
            wide = longin[1, ch, :, group * LANES : (group + 1) * LANES].astype(jnp.float32)
            for m, s in enumerate(horner(wide, start + group * LANES)):
                acc1[group, m] = s
        wait_bytes(halo.at[ch], halo_recv.at[ch])
        spec_h = transform(halo[ch])
        early = short_tile(spec0, spec_h, kept0, spectrum, pl.ds(0, TILE), cols)
        longin[0, ch] = early
        for group in range(2):
            base = start + group * LANES
            wide = longin[0, ch, :, group * LANES : (group + 1) * LANES].astype(jnp.float32)
            for m, s in enumerate(horner(wide, base)):
                weight = jnp.exp(-rate[m : m + 1, pl.ds(base, LANES)] * (7.0 - sub))
                decay = kept1 * z128[m : m + 1, pl.ds(base, LANES)]
                ends0[m : m + 1, pl.ds(base, LANES)] = jnp.sum(s * weight, axis=0, keepdims=True)
                both = (acc1[group, m] + decay * s) * weight
                esend[4 * ch + 2 * group + m // 8, m % 8 : m % 8 + 1, :] = jnp.sum(both, axis=0, keepdims=True)
        for piece in range(4):
            owner = 4 * ch + piece

            @pl.when(owner != me)
            def _():
                pltpu.make_async_remote_copy(
                    src_ref=esend.at[owner], dst_ref=erecv.at[me], send_sem=e_send, recv_sem=e_recv,
                    device_id=(owner, part), device_id_type=MESH).start()

            @pl.when(owner == me)
            def _():
                pltpu.make_async_copy(esend.at[owner], erecv.at[me], e_recv).start()

        return carry

    lax.fori_loop(0, chunks, forward_chunk, 0)

    def inside_chunk(ch, carry):
        start = pl.multiple_of(ch * WIDE, WIDE)
        highs, lows = [], []
        for group in range(2):
            base = start + group * LANES
            lanes = pl.ds(base, LANES)
            power_of = [amp[m : m + 1, lanes] * zb[m, :, lanes] for m in range(MODES)]
            steps = [z8[m : m + 1, lanes] for m in range(MODES)]
            pieces = []
            for block in range(TILE // 8):
                total = power_of[0]
                for p in power_of[1:]:
                    total = total + p
                pieces.append(total)
                if block < TILE // 8 - 1:
                    power_of = [p * z for p, z in zip(power_of, steps)]
            lag_taps = jnp.concatenate(pieces, axis=0)
            high = lag_taps.astype(jnp.bfloat16)
            highs.append(high)
            lows.append((lag_taps - high.astype(jnp.float32)).astype(jnp.bfloat16))
        high = jnp.concatenate(highs, axis=1)
        low = jnp.concatenate(lows, axis=1)
        stacked = jnp.concatenate([high, high, low], axis=0)
        spectrum = jnp.dot(ahead[...], stacked, preferred_element_type=jnp.float32)
        s_real, s_imag = spectrum[:TILE], spectrum[TILE:]
        for half in range(2):
            spec = transform(longin[half, ch])
            real, imag = spec[:TILE], spec[TILE:]
            inside[half, ch] = untransform(real * s_real - imag * s_imag, real * s_imag + imag * s_real)
        return carry

    lax.fori_loop(0, chunks, inside_chunk, 0)

    wait_bytes(erecv, e_recv)
    my_chip = me // 2
    my_cols = pl.ds(pl.multiple_of(my_chip * LANES, LANES), LANES)
    my_rate = rate[pl.ds(pl.multiple_of(8 * lax.rem(me, 2), 8), 8), my_cols]
    block_decay = jnp.exp(-2.0 * TILE * my_rate)

    def scan_step(n, state):
        ssend[n] = state
        before = docs[jnp.maximum(2 * n - 1, 0)]
        through = jnp.where(jnp.logical_and(n > 0, before == docs[2 * n + 1]), 1.0, 0.0).astype(jnp.float32)
        return (block_decay * through) * state + erecv[n]

    lax.fori_loop(0, seq_count, scan_step, jnp.zeros((8, LANES), jnp.float32))

    slot = me // 4

    def hand_back(step, carry):
        target = lax.rem(me + step, seq_count)
        pltpu.make_async_remote_copy(
            src_ref=ssend.at[target], dst_ref=srecv.at[me], send_sem=s_send, recv_sem=s_recv.at[slot],
            device_id=(target, part), device_id_type=MESH).start()
        return carry

    lax.fori_loop(1, seq_count, hand_back, 0)
    pltpu.make_async_copy(ssend.at[me], srecv.at[me], s_recv.at[slot]).start()

    power[...] = jnp.zeros_like(power)

    def outward_chunk(ch, carry):
        start = pl.multiple_of(ch * WIDE, WIDE)
        tiles = pl.ds(pl.multiple_of(4 * ch, 4), 4)
        wait_bytes(srecv.at[tiles], s_recv.at[ch])
        for group in range(2):
            base = start + group * LANES
            lanes = pl.ds(base, LANES)
            steps = [z8[m : m + 1, lanes] for m in range(MODES)]
            states = [kept0 * srecv[4 * ch + 2 * group + m // 8, m % 8 : m % 8 + 1, :] for m in range(MODES)]
            for half in range(2):
                if half == 1:
                    states = [
                        kept1 * (z128[m : m + 1, lanes] * s + ends0[m : m + 1, lanes])
                        for m, s in enumerate(states)
                    ]
                waves = []
                for m, s in enumerate(states):
                    first_step = jnp.exp(-rate[m : m + 1, lanes])
                    waves.append((amp[m : m + 1, lanes] * first_step * s) * zb[m, :, lanes])
                for block in range(TILE // 8):
                    total = inside[half, ch, 8 * block : 8 * block + 8, group * LANES : (group + 1) * LANES]
                    for w in waves:
                        total = total + w
                    rows = pl.ds(half * TILE + 8 * block, 8)
                    total = total * q2[rows, lanes].astype(jnp.float32)
                    longout[rows, lanes] = total
                    power[rows, :] = power[rows, :] + total * total
                    if block < TILE // 8 - 1:
                        waves = [w * z for w, z in zip(waves, steps)]
        return carry

    lax.fori_loop(0, chunks, outward_chunk, 0)

    psend[...] = jnp.zeros_like(psend)
    for half in range(2):
        turned = power[half * TILE : (half + 1) * TILE, :].T
        psend[half : half + 1, :] = jnp.sum(turned, axis=0, keepdims=True)
    for step in range(1, mp_count):
        pltpu.make_async_remote_copy(
            src_ref=psend, dst_ref=precv.at[part], send_sem=p_send, recv_sem=p_recv,
            device_id=(me, lax.rem(part + step, mp_count)), device_id_type=MESH).start()
    precv[part] = psend[...]
    others = pl.ds(0, mp_count - 1)
    wait_bytes(precv.at[others], p_recv)
    total = precv[0]
    for n in range(1, mp_count):
        total = total + precv[n]
    scale = lax.rsqrt(total / (channels * mp_count) + norm_eps)
    for half in range(2):
        column = jnp.broadcast_to(scale[half : half + 1, :], (TILE, LANES)).T
        rows = pl.ds(half * TILE, TILE)
        for group in range(channels // LANES):
            lanes = slice(group * LANES, (group + 1) * LANES)
            outbuf[rows, lanes] = (longout[rows, lanes] * column).astype(jnp.bfloat16)
        pltpu.make_async_copy(outbuf.at[rows], out_h.at[rows], out_sem.at[half]).start()

    for half in range(2):
        rows = pl.ds(half * TILE, TILE)
        pltpu.make_async_copy(outbuf.at[rows], out_h.at[rows], out_sem.at[half]).wait()
    wait_bytes(gated.at[1], halo_send)
    wait_bytes(esend.at[pl.ds(0, seq_count - 1)], e_send)
    wait_bytes(ssend.at[pl.ds(0, seq_count - 1)], s_send)
    wait_bytes(precv.at[others], p_send)


def on_device(mesh_sizes, values, k_first, q_first, k_second, q_second, mr_taps, li_rate, li_residue, tile_docs):
    seq_count, mp_count = mesh_sizes
    rows, channels = values.shape
    chunks = channels // WIDE
    ahead, back = dft_tables()
    f32, bf16 = jnp.float32, jnp.bfloat16
    vmem = pltpu.VMEM
    any_spec = pl.BlockSpec(memory_space=pl.ANY)
    big = vmem((rows, channels), bf16)
    dma = pltpu.SemaphoreType.DMA
    return pl.pallas_call(
        functools.partial(kernel, seq_count, mp_count),
        out_shape=jax.ShapeDtypeStruct((rows, channels), bf16),
        in_specs=[pl.BlockSpec(memory_space=pltpu.SMEM)] + [any_spec] * 10,
        out_specs=any_spec,
        scratch_shapes=[
            big, big, big, big, big,
            vmem((TILE, channels), bf16),
            vmem((MODES, channels), f32),
            vmem((MODES, channels), f32),
            vmem(ahead.shape, bf16),
            vmem(back.shape, bf16),
            vmem((2, chunks, TILE, WIDE), bf16),
            vmem((chunks, TILE, WIDE), bf16),
            vmem((2, chunks, TILE, WIDE), bf16),
            vmem((2, chunks, TILE, WIDE), f32),
            vmem((rows, channels), f32),
            vmem((MODES, channels), f32),
            vmem((MODES, channels), f32),
            vmem((MODES, channels), f32),
            vmem((MODES, 8, channels), f32),
            vmem((2, MODES, 8, LANES), f32),
            vmem((MODES, channels), f32),
            vmem((seq_count, 8, LANES), f32),
            vmem((seq_count, 8, LANES), f32),
            vmem((seq_count, 8, LANES), f32),
            vmem((seq_count, 8, LANES), f32),
            vmem((rows, LANES), f32),
            vmem((8, LANES), f32),
            vmem((mp_count, 8, LANES), f32),
            big,
            dma((2, chunks)),
            dma((8,)),
            dma,
            dma((chunks,)),
            dma, dma, dma,
            dma((chunks,)),
            dma, dma,
            dma((2,)),
        ],
        compiler_params=pltpu.CompilerParams(
            collective_id=0, has_side_effects=True, vmem_limit_bytes=60 * 1024 * 1024),
    )(tile_docs, values, k_first, q_first, k_second, q_second, mr_taps, li_rate, li_residue,
      jnp.asarray(ahead), jnp.asarray(back))


def solution(mesh):
    sizes = (mesh.shape["seq"], mesh.shape["mp"])
    block = P("seq", "mp")
    param = P(None, "mp")
    return jax.shard_map(
        functools.partial(on_device, sizes),
        mesh=mesh,
        in_specs=(block, block, block, block, block, param, param, param, P()),
        out_specs=block,
        check_vma=False,
    )
```

time: 761 us -> 44 us (0.06)
  the two profiles are of different devices: /device:TPU:2 before, /device:TPU:1 now
where the time goes in v1:
time: 44 us; the launch traced here: 43.9 us
  Pallas kernels  41.5 us (94%)
  local copies, waits for them, and re-layouts  2.3 us (5%)
    pallas_call x1, Pallas kernels, on_device(): pl.pallas_call(functools.partial(kernel, seq_count, mp_count), out_shape=...  41.5 us
    unnamed x1, local copies, waits for them, and re-layouts  2.3 us

profile of v1, /device:TPU:1, one launch (start us, length us, event | category | flops | bytes accessed | tf_op | source)
XLA Modules:
  0.0 43.9 jit_solution(712399409481748625)
XLA Ops:
  0.0 41.5 %shard_map.109 = bf16[256,2048]{1,0:T(8,128)(2,1)} custom-call(s32[64]{0:T(128)} %docs.1, bf16[256,2048]{1,0:T(8,128)(2,1)} %values_h.1, bf16[256,2048]{1,0:T(8,128)(2,1)} %k1_h.1, bf16[256,2048]{1,0:T(8,128)(2,1)} %q1_h.1, bf16[256,2048]{1,0:T(8,128)(2,1)} %k2_h.1, bf16[256,2048]{1,0:T(8,128)(2,1)} %q2_h.1, bf16[128,2048]{1,0:T(8,128)(2,1)} %taps_h.1, ...), custom_call_target="tpu_custom_call" | custom-call | tf_op jit(solution)/shard_map/pallas_call | solution.py:329
  41.5 2.3 %copy.13 = bf16[256,2048]{1,0:T(8,128)(2,1)} copy(bf16[256,2048]{1,0:T(8,128)(2,1)} %shard_map.109) | data formatting | bytes 2097152

commit v2 on v1

v2 whole, which is shorter than its diff:
```python
import functools
import jax
import jax.numpy as jnp
import numpy as np
from jax import lax
from jax.experimental import pallas as pl
from jax.experimental.pallas import tpu as pltpu
from jax.sharding import PartitionSpec as P

TILE = 128
MODES = 16
LANES = 128
WIDE = 256
norm_eps = 1e-06
MESH = pl.DeviceIdType.MESH


def split_bf16(table):
    high = table.astype(jnp.bfloat16)
    low = (table - high.astype(np.float64)).astype(jnp.bfloat16)
    return np.asarray(high), np.asarray(low)


def dft_tables():
    freq = 2.0 * np.pi * (4.0 * np.arange(TILE) + 1.0) / (4.0 * TILE)
    angle = freq[:, None] * np.arange(TILE)[None, :]
    real, imag = np.cos(angle), -np.sin(angle)

    def mixed(top, bottom):
        blocks = [part.reshape(TILE // 16, 1, 16, TILE) for part in (top, bottom)]
        return np.concatenate(blocks, axis=1).reshape(2 * TILE, TILE)

    current = mixed(real, imag)
    c_high, c_low = split_bf16(current)
    p_high, p_low = split_bf16(mixed(-imag, real))
    g_high, g_low = split_bf16(current.T / TILE)
    ahead = np.concatenate([c_high, c_low, c_high], axis=1)
    pair = np.concatenate([c_high, p_high, c_low, p_low], axis=1)
    back = np.concatenate([g_high, g_low, g_high], axis=1)
    return ahead, pair, back


def wait_bytes(ref, sem):
    pltpu.make_async_copy(ref, ref, sem).wait()


def parts_of(spectrum):
    blocks = spectrum.reshape(TILE // 16, 2, 16, WIDE)
    return blocks[:, 0], blocks[:, 1]


def woven(real, imag):
    return jnp.stack([real, imag], axis=1).reshape(2 * TILE, WIDE)


def kernel(
    seq_count, mp_count,
    docs, values_h, k1_h, q1_h, k2_h, q2_h, taps_h, rate_h, resid_h, ahead_h, pair_h, back_h,
    outbuf,
    values, k1, q1, k2, q2, taps, rate, resid, ahead, pair, back,
    gated, masked, halo, longin, inside, longout, amp, z1, z8, z128, zb, zr,
    spectra, ends0, ends1, esend, erecv, ssend, srecv, power, psend, precv,
    in_sem, par_sem, halo_send, halo_recv, e_send, e_recv, s_send, s_recv, p_send, p_recv,
):
    me = lax.axis_index("seq")
    part = lax.axis_index("mp")
    channels = values.shape[1]
    chunks = channels // WIDE

    def in_copy(source, target, row, ch):
        cols = pl.ds(ch * WIDE, WIDE)
        return pltpu.make_async_copy(source.at[:, cols], target.at[:, cols], in_sem.at[row, ch])

    for ch in range(chunks):
        in_copy(values_h, values, 0, ch).start()
        in_copy(k1_h, k1, 1, ch).start()

    barrier = pltpu.get_barrier_semaphore()

    def greet(step, carry):
        pl.semaphore_signal(barrier, inc=1, device_id=(lax.rem(me + step, seq_count), part), device_id_type=MESH)
        return carry

    lax.fori_loop(1, seq_count, greet, 0)
    for step in range(1, mp_count):
        pl.semaphore_signal(barrier, inc=1, device_id=(me, lax.rem(part + step, mp_count)), device_id_type=MESH)

    whole = [(rate_h, rate), (resid_h, resid), (taps_h, taps), (ahead_h, ahead), (pair_h, pair), (back_h, back),
             (q1_h, q1), (k2_h, k2), (q2_h, q2)]
    whole_copies = [pltpu.make_async_copy(a, b, par_sem.at[n]) for n, (a, b) in enumerate(whole)]
    for copy in whole_copies:
        copy.start()

    first = 2 * me
    doc_a = docs[first]
    doc_b = docs[first + 1]

    def flag(test):
        return jnp.where(test, 1.0, 0.0).astype(jnp.float32)

    kept0 = flag(jnp.logical_and(me > 0, docs[jnp.maximum(first - 1, 0)] == doc_a))
    kept1 = flag(doc_a == doc_b)
    doc_after = docs[jnp.minimum(first + 2, 2 * seq_count - 1)]
    kept2 = flag(jnp.logical_and(me < seq_count - 1, doc_after == doc_b))

    for ch in range(chunks):
        in_copy(values_h, values, 0, ch).wait()
        in_copy(k1_h, k1, 1, ch).wait()
        cols = pl.ds(ch * WIDE, WIDE)
        rows = pl.ds(TILE, TILE)
        product = k1[rows, cols].astype(jnp.float32) * values[rows, cols].astype(jnp.float32)
        masked[1, ch] = (kept2 * product).astype(jnp.bfloat16)

    pl.semaphore_wait(barrier, seq_count - 1 + mp_count - 1)
    after = lax.rem(me + 1, seq_count)

    for ch in range(chunks):
        pltpu.make_async_remote_copy(
            src_ref=masked.at[1, ch], dst_ref=halo.at[ch], send_sem=halo_send, recv_sem=halo_recv.at[ch],
            device_id=(after, part), device_id_type=MESH).start()

    for ch in range(chunks):
        cols = pl.ds(ch * WIDE, WIDE)
        for half in (0, 1):
            rows = pl.ds(half * TILE, TILE)
            product = k1[rows, cols].astype(jnp.float32) * values[rows, cols].astype(jnp.float32)
            gated[half, ch] = product.astype(jnp.bfloat16)
            if half == 0:
                masked[0, ch] = (kept1 * product).astype(jnp.bfloat16)

    for copy in whole_copies[:2]:
        copy.wait()
    r_all = rate[...]
    amp[...] = resid[...] * jnp.sqrt(r_all)
    z1[...] = jnp.exp(-r_all)
    z8[...] = jnp.exp(-8.0 * r_all)
    z128[...] = jnp.exp(-float(TILE) * r_all)
    sub = lax.broadcasted_iota(jnp.int32, (8, LANES), 0).astype(jnp.float32)

    def fill_zb(group, carry):
        cols = pl.ds(pl.multiple_of(group * LANES, LANES), LANES)
        for m in range(MODES):
            zb[m, :, cols] = jnp.exp(-rate[m : m + 1, cols] * sub)
            zr[m, :, cols] = jnp.exp(-rate[m : m + 1, cols] * (7.0 - sub))
        return carry

    lax.fori_loop(0, channels // LANES, fill_zb, 0)

    for copy in whole_copies[2:]:
        copy.wait()

    def transform(tile):
        doubled = jnp.concatenate([tile, tile], axis=0)
        return jnp.dot(ahead[:, : 2 * TILE], doubled, preferred_element_type=jnp.float32)

    def convolve(spectrum, filter_spectrum):
        real, imag = parts_of(spectrum)
        s_real, s_imag = parts_of(filter_spectrum)
        product = woven(real * s_real - imag * s_imag, real * s_imag + imag * s_real)
        high = product.astype(jnp.bfloat16)
        low = (product - high.astype(jnp.float32)).astype(jnp.bfloat16)
        return jnp.dot(back[...], jnp.concatenate([high, high, low], axis=0), preferred_element_type=jnp.float32)

    def short_tile(half, ch, current, previous):
        cols = pl.ds(pl.multiple_of(ch * WIDE, WIDE), WIDE)
        rows = pl.ds(half * TILE, TILE)
        stacked = jnp.concatenate([current, previous, current, previous], axis=0)
        spectrum = jnp.dot(pair[...], stacked, preferred_element_type=jnp.float32)
        conv = convolve(spectrum, spectra[ch])
        short = (q1[rows, cols].astype(jnp.float32) * conv).astype(jnp.bfloat16)
        longin[half, ch] = (k2[rows, cols].astype(jnp.float32) * short.astype(jnp.float32)).astype(jnp.bfloat16)

    def tile_ends(half, ch, ends):
        for group in range(WIDE // LANES):
            lanes = pl.ds(pl.multiple_of(ch * WIDE, WIDE) + group * LANES, LANES)
            tile = longin[half, ch, :, group * LANES : (group + 1) * LANES].astype(jnp.float32)
            steps = [z8[m : m + 1, lanes] for m in range(MODES)]
            sums = [tile[0:8]] * MODES
            for block in range(1, TILE // 8):
                row = tile[8 * block : 8 * block + 8]
                sums = [s * z + row for s, z in zip(sums, steps)]
            for m, s in enumerate(sums):
                ends[m : m + 1, lanes] = jnp.sum(s * zr[m, :, lanes], axis=0, keepdims=True)

    def late_conv(ch):
        spectra[ch] = transform(taps[:, pl.ds(pl.multiple_of(ch * WIDE, WIDE), WIDE)])
        short_tile(1, ch, gated[1, ch], masked[0, ch])

    def late_chunk(ch, carry):
        tile_ends(1, ch - 1, ends1)
        late_conv(ch)
        return carry

    late_conv(0)
    lax.fori_loop(1, chunks, late_chunk, 0)
    tile_ends(1, chunks - 1, ends1)

    def early_conv(ch):
        short_tile(0, ch, gated[0, ch], halo[ch])

    def send_ends(ch):
        for piece in range(4):
            owner = 4 * ch + piece
            lanes = pl.ds(pl.multiple_of(ch * WIDE, WIDE) + (piece // 2) * LANES, LANES)
            modes = pl.ds(8 * (piece % 2), 8)
            esend[owner] = ends1[modes, lanes] + kept1 * z128[modes, lanes] * ends0[modes, lanes]
        for piece in range(4):
            owner = 4 * ch + piece

            @pl.when(owner != me)
            def _():
                pltpu.make_async_remote_copy(
                    src_ref=esend.at[owner], dst_ref=erecv.at[me], send_sem=e_send, recv_sem=e_recv,
                    device_id=(owner, part), device_id_type=MESH).start()

    def early_chunk(ch, carry):
        wait_bytes(halo.at[ch], halo_recv.at[ch])
        tile_ends(0, ch - 1, ends0)
        early_conv(ch)
        send_ends(ch - 1)
        return carry

    wait_bytes(halo.at[0], halo_recv.at[0])
    early_conv(0)
    lax.fori_loop(1, chunks, early_chunk, 0)
    tile_ends(0, chunks - 1, ends0)
    send_ends(chunks - 1)
    pltpu.make_async_copy(esend.at[me], erecv.at[me], e_recv).start()

    def inside_chunk(ch, carry):
        start = pl.multiple_of(ch * WIDE, WIDE)
        highs, lows = [], []
        for group in range(2):
            lanes = pl.ds(start + group * LANES, LANES)
            power_of = [amp[m : m + 1, lanes] * zb[m, :, lanes] for m in range(MODES)]
            steps = [z8[m : m + 1, lanes] for m in range(MODES)]
            pieces = []
            for block in range(TILE // 8):
                total = power_of[0]
                for p in power_of[1:]:
                    total = total + p
                pieces.append(total)
                if block < TILE // 8 - 1:
                    power_of = [p * z for p, z in zip(power_of, steps)]
            lag_taps = jnp.concatenate(pieces, axis=0)
            high = lag_taps.astype(jnp.bfloat16)
            highs.append(high)
            lows.append((lag_taps - high.astype(jnp.float32)).astype(jnp.bfloat16))
        high = jnp.concatenate(highs, axis=1)
        low = jnp.concatenate(lows, axis=1)
        stacked = jnp.concatenate([high, high, low], axis=0)
        spectrum = jnp.dot(ahead[...], stacked, preferred_element_type=jnp.float32)
        for half in range(2):
            inside[half, ch] = convolve(transform(longin[half, ch]), spectrum)
        return carry

    lax.fori_loop(0, chunks // 2, inside_chunk, 0)

    wait_bytes(erecv, e_recv)
    my_cols = pl.ds(pl.multiple_of((me // 2) * LANES, LANES), LANES)
    my_rate = rate[pl.ds(pl.multiple_of(8 * lax.rem(me, 2), 8), 8), my_cols]
    block_decay = jnp.exp(-2.0 * TILE * my_rate)

    def scan_step(n, state):
        ssend[n] = state
        through = flag(jnp.logical_and(n > 0, docs[jnp.maximum(2 * n - 1, 0)] == docs[2 * n + 1]))
        return (block_decay * through) * state + erecv[n]

    lax.fori_loop(0, seq_count, scan_step, jnp.zeros((8, LANES), jnp.float32))

    slot = me // 4

    def hand_back(step, carry):
        target = lax.rem(me + step, seq_count)
        pltpu.make_async_remote_copy(
            src_ref=ssend.at[target], dst_ref=srecv.at[me], send_sem=s_send, recv_sem=s_recv.at[slot],
            device_id=(target, part), device_id_type=MESH).start()
        return carry

    lax.fori_loop(1, seq_count, hand_back, 0)
    pltpu.make_async_copy(ssend.at[me], srecv.at[me], s_recv.at[slot]).start()

    lax.fori_loop(chunks // 2, chunks, inside_chunk, 0)

    power[...] = jnp.zeros_like(power)

    def outward_chunk(ch, carry):
        start = pl.multiple_of(ch * WIDE, WIDE)
        tiles = pl.ds(pl.multiple_of(4 * ch, 4), 4)
        wait_bytes(srecv.at[tiles], s_recv.at[ch])
        for group in range(2):
            lanes = pl.ds(start + group * LANES, LANES)
            steps = [z8[m : m + 1, lanes] for m in range(MODES)]
            states = [kept0 * srecv[4 * ch + 2 * group + n] for n in range(2)]
            for half in range(2):
                if half == 1:
                    states = [
                        kept1 * (z128[8 * n : 8 * n + 8, lanes] * s + ends0[8 * n : 8 * n + 8, lanes])
                        for n, s in enumerate(states)
                    ]
                begun = [amp[8 * n : 8 * n + 8, lanes] * z1[8 * n : 8 * n + 8, lanes] * s for n, s in enumerate(states)]
                waves = [begun[m // 8][m % 8 : m % 8 + 1] * zb[m, :, lanes] for m in range(MODES)]
                for block in range(TILE // 8):
                    total = inside[half, ch, 8 * block : 8 * block + 8, group * LANES : (group + 1) * LANES]
                    for w in waves:
                        total = total + w
                    rows = pl.ds(half * TILE + 8 * block, 8)
                    total = total * q2[rows, lanes].astype(jnp.float32)
                    longout[rows, lanes] = total
                    power[rows, :] = power[rows, :] + total * total
                    if block < TILE // 8 - 1:
                        waves = [w * z for w, z in zip(waves, steps)]
        return carry

    lax.fori_loop(0, chunks, outward_chunk, 0)

    psend[...] = jnp.zeros_like(psend)
    for half in range(2):
        turned = power[half * TILE : (half + 1) * TILE, :].T
        psend[half : half + 1, :] = jnp.sum(turned, axis=0, keepdims=True)
    for step in range(1, mp_count):
        pltpu.make_async_remote_copy(
            src_ref=psend, dst_ref=precv.at[part], send_sem=p_send, recv_sem=p_recv,
            device_id=(me, lax.rem(part + step, mp_count)), device_id_type=MESH).start()
    precv[part] = psend[...]
    others = pl.ds(0, mp_count - 1)
    wait_bytes(precv.at[others], p_recv)
    total = precv[0]
    for n in range(1, mp_count):
        total = total + precv[n]
    scale = lax.rsqrt(total / (channels * mp_count) + norm_eps)
    for half in range(2):
        column = jnp.broadcast_to(scale[half : half + 1, :], (TILE, LANES)).T
        rows = pl.ds(half * TILE, TILE)
        for group in range(channels // LANES):
            lanes = slice(group * LANES, (group + 1) * LANES)
            outbuf[rows, lanes] = (longout[rows, lanes] * column).astype(jnp.bfloat16)

    wait_bytes(masked.at[1], halo_send)
    wait_bytes(esend.at[pl.ds(0, seq_count - 1)], e_send)
    wait_bytes(ssend.at[pl.ds(0, seq_count - 1)], s_send)
    wait_bytes(precv.at[others], p_send)


def on_device(mesh_sizes, values, k_first, q_first, k_second, q_second, mr_taps, li_rate, li_residue, tile_docs):
    seq_count, mp_count = mesh_sizes
    rows, channels = values.shape
    chunks = channels // WIDE
    ahead, pair, back = dft_tables()
    f32, bf16 = jnp.float32, jnp.bfloat16
    vmem = pltpu.VMEM
    hbm_spec = pl.BlockSpec(memory_space=pltpu.MemorySpace.HBM)
    big = vmem((rows, channels), bf16)
    modal = vmem((MODES, channels), f32)
    tiles = vmem((seq_count, 8, LANES), f32)
    dma = pltpu.SemaphoreType.DMA
    return pl.pallas_call(
        functools.partial(kernel, seq_count, mp_count),
        out_shape=vmem((rows, channels), bf16),
        in_specs=[pl.BlockSpec(memory_space=pltpu.SMEM)] + [hbm_spec] * 11,
        out_specs=pl.BlockSpec(memory_space=pltpu.VMEM),
        scratch_shapes=[
            big, big, big, big, big,
            vmem((TILE, channels), bf16),
            modal, modal,
            vmem(ahead.shape, bf16),
            vmem(pair.shape, bf16),
            vmem(back.shape, bf16),
            vmem((2, chunks, TILE, WIDE), bf16),
            vmem((2, chunks, TILE, WIDE), bf16),
            vmem((chunks, TILE, WIDE), bf16),
            vmem((2, chunks, TILE, WIDE), bf16),
            vmem((2, chunks, TILE, WIDE), f32),
            vmem((rows, channels), f32),
            modal, modal, modal, modal,
            vmem((MODES, 8, channels), f32),
            vmem((MODES, 8, channels), f32),
            vmem((chunks, 2 * TILE, WIDE), f32),
            modal, modal,
            tiles, tiles, tiles, tiles,
            vmem((rows, LANES), f32),
            vmem((8, LANES), f32),
            vmem((mp_count, 8, LANES), f32),
            dma((2, chunks)),
            dma((9,)),
            dma,
            dma((chunks,)),
            dma, dma, dma,
            dma((chunks,)),
            dma, dma,
        ],
        compiler_params=pltpu.CompilerParams(
            collective_id=0, has_side_effects=True, vmem_limit_bytes=56 * 1024 * 1024),
    )(tile_docs, values, k_first, q_first, k_second, q_second, mr_taps, li_rate, li_residue,
      jnp.asarray(ahead), jnp.asarray(pair), jnp.asarray(back))


def solution(mesh):
    sizes = (mesh.shape["seq"], mesh.shape["mp"])
    block = P("seq", "mp")
    param = P(None, "mp")
    return jax.shard_map(
        functools.partial(on_device, sizes),
        mesh=mesh,
        in_specs=(block, block, block, block, block, param, param, param, P()),
        out_specs=block,
        check_vma=False,
    )
```

time: 44 us -> 35.2 us (0.80)
  Pallas kernels: 41.5 us -> 34.1 us
  local copies, waits for them, and re-layouts: 2.3 us -> 0.97 us
    pallas_call x1, Pallas kernels: 41.5 us -> 34.1 us  [on_device(): pl.pallas_call(functools.partial(kernel, seq_count, mp_count), out_shape=...]
    unnamed x1, local copies, waits for them, and re-layouts: 2.3 us -> 0.97 us
where the time goes in v2:
time: 35.2 us; the launch traced here: 35.1 us
  Pallas kernels  34.1 us (97%)
  local copies, waits for them, and re-layouts  0.97 us (3%)
    pallas_call x1, Pallas kernels, on_device(): pl.pallas_call(functools.partial(kernel, seq_count, mp_count), out_shape=...  34.1 us
    unnamed x1, local copies, waits for them, and re-layouts  0.97 us

profile of v2, /device:TPU:1, one launch (start us, length us, event | category | flops | bytes accessed | tf_op | source)
XLA Modules:
  0.0 35.1 jit_solution(10184132792609101605)
XLA Ops:
  0.0 34.1 %shard_map.118 = bf16[256,2048]{1,0:T(8,128)(2,1)S(1)} custom-call(s32[64]{0:T(128)} %docs.1, bf16[256,2048]{1,0:T(8,128)(2,1)} %values_h.1, bf16[256,2048]{1,0:T(8,128)(2,1)} %k1_h.1, bf16[256,2048]{1,0:T(8,128)(2,1)} %q1_h.1, bf16[256,2048]{1,0:T(8,128)(2,1)} %k2_h.1, bf16[256,2048]{1,0:T(8,128)(2,1)} %q2_h.1, bf16[128,2048]{1,0:T(8,128)(2,1)} %taps_h.1, ...), custom_call_target="tpu_custom_call" | custom-call | tf_op jit(solution)/shard_map/pallas_call | solution.py:357
  34.1 1.0 %copy.14 = bf16[256,2048]{1,0:T(8,128)(2,1)} copy(bf16[256,2048]{1,0:T(8,128)(2,1)S(1)} %shard_map.118) | data formatting | bytes 2097152

commit v3 on v2

--- a/solution.py
+++ b/solution.py
@@ -36,7 +36,7 @@
     g_high, g_low = split_bf16(current.T / TILE)
     ahead = np.concatenate([c_high, c_low, c_high], axis=1)
     pair = np.concatenate([c_high, p_high, c_low, p_low], axis=1)
-    back = np.concatenate([g_high, g_low, g_high], axis=1)
+    back = np.concatenate([g_high, g_low], axis=0)
     return ahead, pair, back
 
 
@@ -58,8 +58,8 @@
     docs, values_h, k1_h, q1_h, k2_h, q2_h, taps_h, rate_h, resid_h, ahead_h, pair_h, back_h,
     outbuf,
     values, k1, q1, k2, q2, taps, rate, resid, ahead, pair, back,
-    gated, masked, halo, longin, inside, longout, amp, z1, z8, z128, zb, zr,
-    spectra, ends0, ends1, esend, erecv, ssend, srecv, power, psend, precv,
+    gated, behind, outgoing, longin, inside, longout, amp, z1, z8, z128, zb, zr,
+    spectra, parts, ends, esend, erecv, ssend, srecv, power, psend, precv,
     in_sem, par_sem, halo_send, halo_recv, e_send, e_recv, s_send, s_recv, p_send, p_recv,
 ):
     me = lax.axis_index("seq")
@@ -109,24 +109,23 @@
         cols = pl.ds(ch * WIDE, WIDE)
         rows = pl.ds(TILE, TILE)
         product = k1[rows, cols].astype(jnp.float32) * values[rows, cols].astype(jnp.float32)
-        masked[1, ch] = (kept2 * product).astype(jnp.bfloat16)
+        gated[1, ch] = product.astype(jnp.bfloat16)
+        outgoing[ch] = (kept2 * product).astype(jnp.bfloat16)
 
     pl.semaphore_wait(barrier, seq_count - 1 + mp_count - 1)
     after = lax.rem(me + 1, seq_count)
 
     for ch in range(chunks):
         pltpu.make_async_remote_copy(
-            src_ref=masked.at[1, ch], dst_ref=halo.at[ch], send_sem=halo_send, recv_sem=halo_recv.at[ch],
+            src_ref=outgoing.at[ch], dst_ref=behind.at[0, ch], send_sem=halo_send, recv_sem=halo_recv.at[ch],
             device_id=(after, part), device_id_type=MESH).start()
 
     for ch in range(chunks):
         cols = pl.ds(ch * WIDE, WIDE)
-        for half in (0, 1):
-            rows = pl.ds(half * TILE, TILE)
-            product = k1[rows, cols].astype(jnp.float32) * values[rows, cols].astype(jnp.float32)
-            gated[half, ch] = product.astype(jnp.bfloat16)
-            if half == 0:
-                masked[0, ch] = (kept1 * product).astype(jnp.bfloat16)
+        rows = pl.ds(0, TILE)
+        product = k1[rows, cols].astype(jnp.float32) * values[rows, cols].astype(jnp.float32)
+        gated[0, ch] = product.astype(jnp.bfloat16)
+        behind[1, ch] = (kept1 * product).astype(jnp.bfloat16)
 
     for copy in whole_copies[:2]:
         copy.wait()
@@ -135,16 +134,16 @@
     z1[...] = jnp.exp(-r_all)
     z8[...] = jnp.exp(-8.0 * r_all)
     z128[...] = jnp.exp(-float(TILE) * r_all)
-    sub = lax.broadcasted_iota(jnp.int32, (8, LANES), 0).astype(jnp.float32)
-
-    def fill_zb(group, carry):
-        cols = pl.ds(pl.multiple_of(group * LANES, LANES), LANES)
+    sub = lax.broadcasted_iota(jnp.int32, (8, WIDE), 0).astype(jnp.float32)
+
+    def fill_zb(ch, carry):
+        cols = pl.ds(pl.multiple_of(ch * WIDE, WIDE), WIDE)
         for m in range(MODES):
             zb[m, :, cols] = jnp.exp(-rate[m : m + 1, cols] * sub)
             zr[m, :, cols] = jnp.exp(-rate[m : m + 1, cols] * (7.0 - sub))
         return carry
 
-    lax.fori_loop(0, channels // LANES, fill_zb, 0)
+    lax.fori_loop(0, chunks, fill_zb, 0)
 
     for copy in whole_copies[2:]:
         copy.wait()
@@ -153,26 +152,48 @@
         doubled = jnp.concatenate([tile, tile], axis=0)
         return jnp.dot(ahead[:, : 2 * TILE], doubled, preferred_element_type=jnp.float32)
 
-    def convolve(spectrum, filter_spectrum):
+    def product_of(spectrum, filter_spectrum):
         real, imag = parts_of(spectrum)
         s_real, s_imag = parts_of(filter_spectrum)
         product = woven(real * s_real - imag * s_imag, real * s_imag + imag * s_real)
         high = product.astype(jnp.bfloat16)
         low = (product - high.astype(jnp.float32)).astype(jnp.bfloat16)
-        return jnp.dot(back[...], jnp.concatenate([high, high, low], axis=0), preferred_element_type=jnp.float32)
-
-    def short_tile(half, ch, current, previous):
-        cols = pl.ds(pl.multiple_of(ch * WIDE, WIDE), WIDE)
-        rows = pl.ds(half * TILE, TILE)
+        return high, low
+
+    def invert(high, low):
+        both = jnp.dot(back[...], high, preferred_element_type=jnp.float32)
+        fine = jnp.dot(back[:TILE], low, preferred_element_type=jnp.float32)
+        return both[:TILE] + (both[TILE:] + fine)
+
+    def convolve(spectrum, filter_spectrum):
+        return invert(*product_of(spectrum, filter_spectrum))
+
+    def place_of(step):
+        half = 1 - step // chunks
+        ch = lax.rem(step, chunks)
+        return half, ch, pl.multiple_of(ch * WIDE, WIDE)
+
+    def begin_tile(step):
+        half, ch, start = place_of(step)
+        current, previous = gated[half, ch], behind[half, ch]
         stacked = jnp.concatenate([current, previous, current, previous], axis=0)
         spectrum = jnp.dot(pair[...], stacked, preferred_element_type=jnp.float32)
-        conv = convolve(spectrum, spectra[ch])
+        return spectrum, spectra[ch]
+
+    def keep_parts(begun):
+        parts[0], parts[1] = product_of(*begun)
+
+    def finish_tile(step, conv):
+        half, ch, start = place_of(step)
+        cols = pl.ds(start, WIDE)
+        rows = pl.ds(pl.multiple_of(half * TILE, TILE), TILE)
         short = (q1[rows, cols].astype(jnp.float32) * conv).astype(jnp.bfloat16)
         longin[half, ch] = (k2[rows, cols].astype(jnp.float32) * short.astype(jnp.float32)).astype(jnp.bfloat16)
 
-    def tile_ends(half, ch, ends):
-        for group in range(WIDE // LANES):
-            lanes = pl.ds(pl.multiple_of(ch * WIDE, WIDE) + group * LANES, LANES)
+    def tile_ends(step, groups):
+        half, ch, start = place_of(step)
+        for group in groups:
+            lanes = pl.ds(start + group * LANES, LANES)
             tile = longin[half, ch, :, group * LANES : (group + 1) * LANES].astype(jnp.float32)
             steps = [z8[m : m + 1, lanes] for m in range(MODES)]
             sums = [tile[0:8]] * MODES
@@ -180,30 +201,18 @@
                 row = tile[8 * block : 8 * block + 8]
                 sums = [s * z + row for s, z in zip(sums, steps)]
             for m, s in enumerate(sums):
-                ends[m : m + 1, lanes] = jnp.sum(s * zr[m, :, lanes], axis=0, keepdims=True)
-
-    def late_conv(ch):
+                ends[half, m : m + 1, lanes] = jnp.sum(s * zr[m, :, lanes], axis=0, keepdims=True)
+
+    def tap_chunk(ch, carry):
         spectra[ch] = transform(taps[:, pl.ds(pl.multiple_of(ch * WIDE, WIDE), WIDE)])
-        short_tile(1, ch, gated[1, ch], masked[0, ch])
-
-    def late_chunk(ch, carry):
-        tile_ends(1, ch - 1, ends1)
-        late_conv(ch)
-        return carry
-
-    late_conv(0)
-    lax.fori_loop(1, chunks, late_chunk, 0)
-    tile_ends(1, chunks - 1, ends1)
-
-    def early_conv(ch):
-        short_tile(0, ch, gated[0, ch], halo[ch])
+        return carry
 
     def send_ends(ch):
         for piece in range(4):
             owner = 4 * ch + piece
             lanes = pl.ds(pl.multiple_of(ch * WIDE, WIDE) + (piece // 2) * LANES, LANES)
             modes = pl.ds(8 * (piece % 2), 8)
-            esend[owner] = ends1[modes, lanes] + kept1 * z128[modes, lanes] * ends0[modes, lanes]
+            esend[owner] = ends[1, modes, lanes] + kept1 * z128[modes, lanes] * ends[0, modes, lanes]
         for piece in range(4):
             owner = 4 * ch + piece
 
@@ -213,17 +222,37 @@
                     src_ref=esend.at[owner], dst_ref=erecv.at[me], send_sem=e_send, recv_sem=e_recv,
                     device_id=(owner, part), device_id_type=MESH).start()
 
-    def early_chunk(ch, carry):
-        wait_bytes(halo.at[ch], halo_recv.at[ch])
-        tile_ends(0, ch - 1, ends0)
-        early_conv(ch)
-        send_ends(ch - 1)
-        return carry
-
-    wait_bytes(halo.at[0], halo_recv.at[0])
-    early_conv(0)
-    lax.fori_loop(1, chunks, early_chunk, 0)
-    tile_ends(0, chunks - 1, ends0)
+    def forward_step(step, carry):
+        @pl.when(step + 1 >= chunks)
+        def _():
+            ch = step + 1 - chunks
+            wait_bytes(behind.at[0, ch], halo_recv.at[ch])
+
+        conv = invert(parts[0], parts[1])
+        tile_ends(step - 1, (0,))
+        finish_tile(step, conv)
+        begun = begin_tile(step + 1)
+        tile_ends(step - 1, (1,))
+        keep_parts(begun)
+
+        @pl.when(step - 1 >= chunks)
+        def _():
+            send_ends(step - 1 - chunks)
+
+        return carry
+
+    lax.fori_loop(0, chunks, tap_chunk, 0)
+    last = 2 * chunks - 1
+    keep_parts(begin_tile(0))
+    first_conv = invert(parts[0], parts[1])
+    keep_parts(begin_tile(1))
+    finish_tile(0, first_conv)
+    lax.fori_loop(1, last, forward_step, 0)
+    last_conv = invert(parts[0], parts[1])
+    tile_ends(last - 1, (0, 1))
+    finish_tile(last, last_conv)
+    send_ends(chunks - 2)
+    tile_ends(last, (0, 1))
     send_ends(chunks - 1)
     pltpu.make_async_copy(esend.at[me], erecv.at[me], e_recv).start()
 
@@ -295,7 +324,7 @@
             for half in range(2):
                 if half == 1:
                     states = [
-                        kept1 * (z128[8 * n : 8 * n + 8, lanes] * s + ends0[8 * n : 8 * n + 8, lanes])
+                        kept1 * (z128[8 * n : 8 * n + 8, lanes] * s + ends[0, 8 * n : 8 * n + 8, lanes])
                         for n, s in enumerate(states)
                     ]
                 begun = [amp[8 * n : 8 * n + 8, lanes] * z1[8 * n : 8 * n + 8, lanes] * s for n, s in enumerate(states)]
@@ -336,7 +365,7 @@
             lanes = slice(group * LANES, (group + 1) * LANES)
             outbuf[rows, lanes] = (longout[rows, lanes] * column).astype(jnp.bfloat16)
 
-    wait_bytes(masked.at[1], halo_send)
+    wait_bytes(outgoing, halo_send)
     wait_bytes(esend.at[pl.ds(0, seq_count - 1)], e_send)
     wait_bytes(ssend.at[pl.ds(0, seq_count - 1)], s_send)
     wait_bytes(precv.at[others], p_send)
@@ -376,7 +405,8 @@
             vmem((MODES, 8, channels), f32),
             vmem((MODES, 8, channels), f32),
             vmem((chunks, 2 * TILE, WIDE), f32),
-            modal, modal,
+            vmem((2, 2 * TILE, WIDE), bf16),
+            vmem((2, MODES, channels), f32),
             tiles, tiles, tiles, tiles,
             vmem((rows, LANES), f32),
             vmem((8, LANES), f32),

time: 35.2 us -> 34.6 us (0.983)
  Pallas kernels: 34.1 us -> 33.5 us
    pallas_call x1, Pallas kernels: 34.1 us -> 33.5 us  [on_device(): pl.pallas_call(functools.partial(kernel, seq_count, mp_count), out_shape=...]
where the time goes in v3:
time: 34.6 us; the launch traced here: 34.5 us
  Pallas kernels  33.5 us (97%)
  local copies, waits for them, and re-layouts  0.97 us (3%)
    pallas_call x1, Pallas kernels, on_device(): pl.pallas_call(functools.partial(kernel, seq_count, mp_count), out_shape=...  33.5 us
    unnamed x1, local copies, waits for them, and re-layouts  0.97 us

profile of v3, /device:TPU:1, one launch (start us, length us, event | category | flops | bytes accessed | tf_op | source)
XLA Modules:
  0.0 34.5 jit_solution(17317578947101565973)
XLA Ops:
  0.0 33.5 %shard_map.118 = bf16[256,2048]{1,0:T(8,128)(2,1)S(1)} custom-call(s32[64]{0:T(128)} %docs.1, bf16[256,2048]{1,0:T(8,128)(2,1)} %values_h.1, bf16[256,2048]{1,0:T(8,128)(2,1)} %k1_h.1, bf16[256,2048]{1,0:T(8,128)(2,1)} %q1_h.1, bf16[256,2048]{1,0:T(8,128)(2,1)} %k2_h.1, bf16[256,2048]{1,0:T(8,128)(2,1)} %q2_h.1, bf16[128,2048]{1,0:T(8,128)(2,1)} %taps_h.1, ...), custom_call_target="tpu_custom_call" | custom-call | tf_op jit(solution)/shard_map/pallas_call | solution.py:386
  33.5 1.0 %copy.14 = bf16[256,2048]{1,0:T(8,128)(2,1)} copy(bf16[256,2048]{1,0:T(8,128)(2,1)S(1)} %shard_map.118) | data formatting | bytes 2097152

commit v4 on v3

--- a/solution.py
+++ b/solution.py
@@ -130,20 +130,17 @@
     for copy in whole_copies[:2]:
         copy.wait()
     r_all = rate[...]
-    amp[...] = resid[...] * jnp.sqrt(r_all)
-    z1[...] = jnp.exp(-r_all)
     z8[...] = jnp.exp(-8.0 * r_all)
     z128[...] = jnp.exp(-float(TILE) * r_all)
     sub = lax.broadcasted_iota(jnp.int32, (8, WIDE), 0).astype(jnp.float32)
 
-    def fill_zb(ch, carry):
+    def fill_zr(ch, carry):
         cols = pl.ds(pl.multiple_of(ch * WIDE, WIDE), WIDE)
         for m in range(MODES):
-            zb[m, :, cols] = jnp.exp(-rate[m : m + 1, cols] * sub)
             zr[m, :, cols] = jnp.exp(-rate[m : m + 1, cols] * (7.0 - sub))
         return carry
 
-    lax.fori_loop(0, chunks, fill_zb, 0)
+    lax.fori_loop(0, chunks, fill_zr, 0)
 
     for copy in whole_copies[2:]:
         copy.wait()
@@ -228,11 +225,10 @@
             ch = step + 1 - chunks
             wait_bytes(behind.at[0, ch], halo_recv.at[ch])
 
+        tile_ends(step - 1, (0, 1))
         conv = invert(parts[0], parts[1])
-        tile_ends(step - 1, (0,))
+        begun = begin_tile(step + 1)
         finish_tile(step, conv)
-        begun = begin_tile(step + 1)
-        tile_ends(step - 1, (1,))
         keep_parts(begun)
 
         @pl.when(step - 1 >= chunks)
@@ -256,8 +252,14 @@
     send_ends(chunks - 1)
     pltpu.make_async_copy(esend.at[me], erecv.at[me], e_recv).start()
 
-    def inside_chunk(ch, carry):
+    amp[...] = resid[...] * jnp.sqrt(rate[...])
+    z1[...] = jnp.exp(-rate[...])
+
+    def inside_chunk(ch):
         start = pl.multiple_of(ch * WIDE, WIDE)
+        cols = pl.ds(start, WIDE)
+        for m in range(MODES):
+            zb[m, :, cols] = jnp.exp(-rate[m : m + 1, cols] * sub)
         highs, lows = [], []
         for group in range(2):
             lanes = pl.ds(start + group * LANES, LANES)
@@ -281,23 +283,16 @@
         spectrum = jnp.dot(ahead[...], stacked, preferred_element_type=jnp.float32)
         for half in range(2):
             inside[half, ch] = convolve(transform(longin[half, ch]), spectrum)
-        return carry
-
-    lax.fori_loop(0, chunks // 2, inside_chunk, 0)
-
-    wait_bytes(erecv, e_recv)
+
     my_cols = pl.ds(pl.multiple_of((me // 2) * LANES, LANES), LANES)
     my_rate = rate[pl.ds(pl.multiple_of(8 * lax.rem(me, 2), 8), 8), my_cols]
     block_decay = jnp.exp(-2.0 * TILE * my_rate)
+    slot = me // 4
 
     def scan_step(n, state):
         ssend[n] = state
         through = flag(jnp.logical_and(n > 0, docs[jnp.maximum(2 * n - 1, 0)] == docs[2 * n + 1]))
         return (block_decay * through) * state + erecv[n]
-
-    lax.fori_loop(0, seq_count, scan_step, jnp.zeros((8, LANES), jnp.float32))
-
-    slot = me // 4
 
     def hand_back(step, carry):
         target = lax.rem(me + step, seq_count)
@@ -306,10 +301,18 @@
             device_id=(target, part), device_id_type=MESH).start()
         return carry
 
-    lax.fori_loop(1, seq_count, hand_back, 0)
-    pltpu.make_async_copy(ssend.at[me], srecv.at[me], s_recv.at[slot]).start()
-
-    lax.fori_loop(chunks // 2, chunks, inside_chunk, 0)
+    def middle_chunk(ch, carry):
+        @pl.when(ch == 2 + slot // 2)
+        def _():
+            wait_bytes(erecv, e_recv)
+            lax.fori_loop(0, seq_count, scan_step, jnp.zeros((8, LANES), jnp.float32), unroll=8)
+            lax.fori_loop(1, seq_count, hand_back, 0)
+            pltpu.make_async_copy(ssend.at[me], srecv.at[me], s_recv.at[slot]).start()
+
+        inside_chunk(ch)
+        return carry
+
+    lax.fori_loop(0, chunks, middle_chunk, 0)
 
     power[...] = jnp.zeros_like(power)
 

time: 34.6 us -> 34.1 us (0.986)
  Pallas kernels: 33.5 us -> 33 us
    pallas_call x1, Pallas kernels: 33.5 us -> 33 us  [on_device(): pl.pallas_call(functools.partial(kernel, seq_count, mp_count), out_shape=...]
where the time goes in v4:
time: 34.1 us; the launch traced here: 33.9 us
  Pallas kernels  33 us (97%)
  local copies, waits for them, and re-layouts  0.97 us (3%)
    pallas_call x1, Pallas kernels, on_device(): pl.pallas_call(functools.partial(kernel, seq_count, mp_count), out_shape=...  33 us
    unnamed x1, local copies, waits for them, and re-layouts  0.97 us

profile of v4, /device:TPU:1, one launch (start us, length us, event | category | flops | bytes accessed | tf_op | source)
XLA Modules:
  0.0 33.9 jit_solution(6788449769015409928)
XLA Ops:
  0.0 33.0 %shard_map.118 = bf16[256,2048]{1,0:T(8,128)(2,1)S(1)} custom-call(s32[64]{0:T(128)} %docs.1, bf16[256,2048]{1,0:T(8,128)(2,1)} %values_h.1, bf16[256,2048]{1,0:T(8,128)(2,1)} %k1_h.1, bf16[256,2048]{1,0:T(8,128)(2,1)} %q1_h.1, bf16[256,2048]{1,0:T(8,128)(2,1)} %k2_h.1, bf16[256,2048]{1,0:T(8,128)(2,1)} %q2_h.1, bf16[128,2048]{1,0:T(8,128)(2,1)} %taps_h.1, ...), custom_call_target="tpu_custom_call" | custom-call | tf_op jit(solution)/shard_map/pallas_call | solution.py:389
  33.0 1.0 %copy.14 = bf16[256,2048]{1,0:T(8,128)(2,1)} copy(bf16[256,2048]{1,0:T(8,128)(2,1)S(1)} %shard_map.118) | data formatting | bytes 2097152

commit v5 on v4

--- a/solution.py
+++ b/solution.py
@@ -59,7 +59,7 @@
     outbuf,
     values, k1, q1, k2, q2, taps, rate, resid, ahead, pair, back,
     gated, behind, outgoing, longin, inside, longout, amp, z1, z8, z128, zb, zr,
-    spectra, parts, ends, esend, erecv, ssend, srecv, power, psend, precv,
+    spectra, parts, lag, ends, esend, erecv, ssend, srecv, power, psend, precv,
     in_sem, par_sem, halo_send, halo_recv, e_send, e_recv, s_send, s_recv, p_send, p_recv,
 ):
     me = lax.axis_index("seq")
@@ -71,6 +71,10 @@
         cols = pl.ds(ch * WIDE, WIDE)
         return pltpu.make_async_copy(source.at[:, cols], target.at[:, cols], in_sem.at[row, ch])
 
+    whole = [(rate_h, rate), (resid_h, resid), (taps_h, taps), (ahead_h, ahead), (pair_h, pair), (back_h, back),
+             (q1_h, q1), (k2_h, k2), (q2_h, q2)]
+    whole_copies = [pltpu.make_async_copy(a, b, par_sem.at[n]) for n, (a, b) in enumerate(whole)]
+    whole_copies[0].start()
     for ch in range(chunks):
         in_copy(values_h, values, 0, ch).start()
         in_copy(k1_h, k1, 1, ch).start()
@@ -85,10 +89,7 @@
     for step in range(1, mp_count):
         pl.semaphore_signal(barrier, inc=1, device_id=(me, lax.rem(part + step, mp_count)), device_id_type=MESH)
 
-    whole = [(rate_h, rate), (resid_h, resid), (taps_h, taps), (ahead_h, ahead), (pair_h, pair), (back_h, back),
-             (q1_h, q1), (k2_h, k2), (q2_h, q2)]
-    whole_copies = [pltpu.make_async_copy(a, b, par_sem.at[n]) for n, (a, b) in enumerate(whole)]
-    for copy in whole_copies:
+    for copy in whole_copies[1:]:
         copy.start()
 
     first = 2 * me
@@ -102,6 +103,20 @@
     kept1 = flag(doc_a == doc_b)
     doc_after = docs[jnp.minimum(first + 2, 2 * seq_count - 1)]
     kept2 = flag(jnp.logical_and(me < seq_count - 1, doc_after == doc_b))
+
+    whole_copies[0].wait()
+    r_all = rate[...]
+    z8[...] = jnp.exp(-8.0 * r_all)
+    z128[...] = jnp.exp(-float(TILE) * r_all)
+    sub = lax.broadcasted_iota(jnp.int32, (8, WIDE), 0).astype(jnp.float32)
+
+    def fill_zr(ch, carry):
+        cols = pl.ds(pl.multiple_of(ch * WIDE, WIDE), WIDE)
+        for m in range(MODES):
+            zr[m, :, cols] = jnp.exp(-rate[m : m + 1, cols] * (7.0 - sub))
+        return carry
+
+    lax.fori_loop(0, chunks, fill_zr, 0)
 
     for ch in range(chunks):
         in_copy(values_h, values, 0, ch).wait()
@@ -127,22 +142,7 @@
         gated[0, ch] = product.astype(jnp.bfloat16)
         behind[1, ch] = (kept1 * product).astype(jnp.bfloat16)
 
-    for copy in whole_copies[:2]:
-        copy.wait()
-    r_all = rate[...]
-    z8[...] = jnp.exp(-8.0 * r_all)
-    z128[...] = jnp.exp(-float(TILE) * r_all)
-    sub = lax.broadcasted_iota(jnp.int32, (8, WIDE), 0).astype(jnp.float32)
-
-    def fill_zr(ch, carry):
-        cols = pl.ds(pl.multiple_of(ch * WIDE, WIDE), WIDE)
-        for m in range(MODES):
-            zr[m, :, cols] = jnp.exp(-rate[m : m + 1, cols] * (7.0 - sub))
-        return carry
-
-    lax.fori_loop(0, chunks, fill_zr, 0)
-
-    for copy in whole_copies[2:]:
+    for copy in whole_copies[1:]:
         copy.wait()
 
     def transform(tile):
@@ -255,7 +255,7 @@
     amp[...] = resid[...] * jnp.sqrt(rate[...])
     z1[...] = jnp.exp(-rate[...])
 
-    def inside_chunk(ch):
+    def lag_taps(ch):
         start = pl.multiple_of(ch * WIDE, WIDE)
         cols = pl.ds(start, WIDE)
         for m in range(MODES):
@@ -273,17 +273,34 @@
                 pieces.append(total)
                 if block < TILE // 8 - 1:
                     power_of = [p * z for p, z in zip(power_of, steps)]
-            lag_taps = jnp.concatenate(pieces, axis=0)
-            high = lag_taps.astype(jnp.bfloat16)
+            wide = jnp.concatenate(pieces, axis=0)
+            high = wide.astype(jnp.bfloat16)
             highs.append(high)
-            lows.append((lag_taps - high.astype(jnp.float32)).astype(jnp.bfloat16))
-        high = jnp.concatenate(highs, axis=1)
-        low = jnp.concatenate(lows, axis=1)
+            lows.append((wide - high.astype(jnp.float32)).astype(jnp.bfloat16))
+        return jnp.concatenate(highs, axis=1), jnp.concatenate(lows, axis=1)
+
+    def products(ch, high, low):
         stacked = jnp.concatenate([high, high, low], axis=0)
         spectrum = jnp.dot(ahead[...], stacked, preferred_element_type=jnp.float32)
+        return [product_of(transform(longin[half, ch]), spectrum) for half in range(2)]
+
+    def keep_products(made):
         for half in range(2):
-            inside[half, ch] = convolve(transform(longin[half, ch]), spectrum)
-
+            parts[2 * half], parts[2 * half + 1] = made[half]
+
+    def inside_chunk(ch):
+        high, low = lag[0], lag[1]
+        following = lag_taps(jnp.minimum(ch + 2, chunks - 1))
+        done = [invert(parts[2 * half], parts[2 * half + 1]) for half in range(2)]
+        made = products(jnp.minimum(ch + 1, chunks - 1), high, low)
+        for half in range(2):
+            inside[half, ch] = done[half]
+        keep_products(made)
+        lag[0], lag[1] = following
+
+    opening = lag_taps(0)
+    lag[0], lag[1] = lag_taps(1)
+    keep_products(products(0, *opening))
     my_cols = pl.ds(pl.multiple_of((me // 2) * LANES, LANES), LANES)
     my_rate = rate[pl.ds(pl.multiple_of(8 * lax.rem(me, 2), 8), 8), my_cols]
     block_decay = jnp.exp(-2.0 * TILE * my_rate)
@@ -302,7 +319,7 @@
         return carry
 
     def middle_chunk(ch, carry):
-        @pl.when(ch == 2 + slot // 2)
+        @pl.when(ch == 1 + (slot + 1) // 2)
         def _():
             wait_bytes(erecv, e_recv)
             lax.fori_loop(0, seq_count, scan_step, jnp.zeros((8, LANES), jnp.float32), unroll=8)
@@ -408,7 +425,8 @@
             vmem((MODES, 8, channels), f32),
             vmem((MODES, 8, channels), f32),
             vmem((chunks, 2 * TILE, WIDE), f32),
-            vmem((2, 2 * TILE, WIDE), bf16),
+            vmem((4, 2 * TILE, WIDE), bf16),
+            vmem((2, TILE, WIDE), bf16),
             vmem((2, MODES, channels), f32),
             tiles, tiles, tiles, tiles,
             vmem((rows, LANES), f32),

time: 34.1 us -> 34.3 us (level)
  no operation moved by 1% of the time
where the time goes in v5:
time: 34.3 us; the launch traced here: 34.2 us
  Pallas kernels  33.2 us (97%)
  local copies, waits for them, and re-layouts  0.97 us (3%)
    pallas_call x1, Pallas kernels, on_device(): pl.pallas_call(functools.partial(kernel, seq_count, mp_count), out_shape=...  33.2 us
    unnamed x1, local copies, waits for them, and re-layouts  0.97 us

profile of v5, /device:TPU:1, one launch (start us, length us, event | category | flops | bytes accessed | tf_op | source)
XLA Modules:
  0.0 34.2 jit_solution(5346338276980268394)
XLA Ops:
  0.0 33.2 %shard_map.118 = bf16[256,2048]{1,0:T(8,128)(2,1)S(1)} custom-call(s32[64]{0:T(128)} %docs.1, bf16[256,2048]{1,0:T(8,128)(2,1)} %values_h.1, bf16[256,2048]{1,0:T(8,128)(2,1)} %k1_h.1, bf16[256,2048]{1,0:T(8,128)(2,1)} %q1_h.1, bf16[256,2048]{1,0:T(8,128)(2,1)} %k2_h.1, bf16[256,2048]{1,0:T(8,128)(2,1)} %q2_h.1, bf16[128,2048]{1,0:T(8,128)(2,1)} %taps_h.1, ...), custom_call_target="tpu_custom_call" | custom-call | tf_op jit(solution)/shard_map/pallas_call | solution.py:406
  33.2 1.0 %copy.14 = bf16[256,2048]{1,0:T(8,128)(2,1)} copy(bf16[256,2048]{1,0:T(8,128)(2,1)S(1)} %shard_map.118) | data formatting | bytes 2097152

commit v6 on v5

--- a/solution.py
+++ b/solution.py
@@ -58,8 +58,8 @@
     docs, values_h, k1_h, q1_h, k2_h, q2_h, taps_h, rate_h, resid_h, ahead_h, pair_h, back_h,
     outbuf,
     values, k1, q1, k2, q2, taps, rate, resid, ahead, pair, back,
-    gated, behind, outgoing, longin, inside, longout, amp, z1, z8, z128, zb, zr,
-    spectra, parts, lag, ends, esend, erecv, ssend, srecv, power, psend, precv,
+    tiles, longin, inside, longout, amp, z1, z8, z128, zb, zr,
+    spectra, parts, lag, pairs, ends, esend, erecv, ssend, srecv, power, psend, precv,
     in_sem, par_sem, halo_send, halo_recv, e_send, e_recv, s_send, s_recv, p_send, p_recv,
 ):
     me = lax.axis_index("seq")
@@ -101,8 +101,6 @@
 
     kept0 = flag(jnp.logical_and(me > 0, docs[jnp.maximum(first - 1, 0)] == doc_a))
     kept1 = flag(doc_a == doc_b)
-    doc_after = docs[jnp.minimum(first + 2, 2 * seq_count - 1)]
-    kept2 = flag(jnp.logical_and(me < seq_count - 1, doc_after == doc_b))
 
     whole_copies[0].wait()
     r_all = rate[...]
@@ -124,26 +122,29 @@
         cols = pl.ds(ch * WIDE, WIDE)
         rows = pl.ds(TILE, TILE)
         product = k1[rows, cols].astype(jnp.float32) * values[rows, cols].astype(jnp.float32)
-        gated[1, ch] = product.astype(jnp.bfloat16)
-        outgoing[ch] = (kept2 * product).astype(jnp.bfloat16)
+        tiles[2, ch] = product.astype(jnp.bfloat16)
 
     pl.semaphore_wait(barrier, seq_count - 1 + mp_count - 1)
     after = lax.rem(me + 1, seq_count)
 
     for ch in range(chunks):
         pltpu.make_async_remote_copy(
-            src_ref=outgoing.at[ch], dst_ref=behind.at[0, ch], send_sem=halo_send, recv_sem=halo_recv.at[ch],
+            src_ref=tiles.at[2, ch], dst_ref=tiles.at[0, ch], send_sem=halo_send, recv_sem=halo_recv.at[ch],
             device_id=(after, part), device_id_type=MESH).start()
 
     for ch in range(chunks):
         cols = pl.ds(ch * WIDE, WIDE)
         rows = pl.ds(0, TILE)
         product = k1[rows, cols].astype(jnp.float32) * values[rows, cols].astype(jnp.float32)
-        gated[0, ch] = product.astype(jnp.bfloat16)
-        behind[1, ch] = (kept1 * product).astype(jnp.bfloat16)
+        tiles[1, ch] = product.astype(jnp.bfloat16)
 
     for copy in whole_copies[1:]:
         copy.wait()
+    for half, kept in enumerate((kept0, kept1)):
+        for n in range(4):
+            cols = slice(n * TILE, (n + 1) * TILE)
+            block = pair[:, cols]
+            pairs[half, :, cols] = (kept * block.astype(jnp.float32)).astype(jnp.bfloat16) if n % 2 else block
 
     def transform(tile):
         doubled = jnp.concatenate([tile, tile], axis=0)
@@ -172,9 +173,9 @@
 
     def begin_tile(step):
         half, ch, start = place_of(step)
-        current, previous = gated[half, ch], behind[half, ch]
+        current, previous = tiles[half + 1, ch], tiles[half, ch]
         stacked = jnp.concatenate([current, previous, current, previous], axis=0)
-        spectrum = jnp.dot(pair[...], stacked, preferred_element_type=jnp.float32)
+        spectrum = jnp.dot(pairs[half], stacked, preferred_element_type=jnp.float32)
         return spectrum, spectra[ch]
 
     def keep_parts(begun):
@@ -219,17 +220,20 @@
                     src_ref=esend.at[owner], dst_ref=erecv.at[me], send_sem=e_send, recv_sem=e_recv,
                     device_id=(owner, part), device_id_type=MESH).start()
 
-    def forward_step(step, carry):
-        @pl.when(step + 1 >= chunks)
-        def _():
-            ch = step + 1 - chunks
-            wait_bytes(behind.at[0, ch], halo_recv.at[ch])
-
+    def side_by_side(step):
         tile_ends(step - 1, (0, 1))
         conv = invert(parts[0], parts[1])
         begun = begin_tile(step + 1)
         finish_tile(step, conv)
         keep_parts(begun)
+
+    def forward_step(step, carry):
+        @pl.when(step + 1 >= chunks)
+        def _():
+            ch = step + 1 - chunks
+            wait_bytes(tiles.at[0, ch], halo_recv.at[ch])
+
+        side_by_side(step)
 
         @pl.when(step - 1 >= chunks)
         def _():
@@ -291,8 +295,8 @@
     def inside_chunk(ch):
         high, low = lag[0], lag[1]
         following = lag_taps(jnp.minimum(ch + 2, chunks - 1))
+        made = products(jnp.minimum(ch + 1, chunks - 1), high, low)
         done = [invert(parts[2 * half], parts[2 * half + 1]) for half in range(2)]
-        made = products(jnp.minimum(ch + 1, chunks - 1), high, low)
         for half in range(2):
             inside[half, ch] = done[half]
         keep_products(made)
@@ -319,7 +323,7 @@
         return carry
 
     def middle_chunk(ch, carry):
-        @pl.when(ch == 1 + (slot + 1) // 2)
+        @pl.when(ch == 2 + slot // 2)
         def _():
             wait_bytes(erecv, e_recv)
             lax.fori_loop(0, seq_count, scan_step, jnp.zeros((8, LANES), jnp.float32), unroll=8)
@@ -335,8 +339,8 @@
 
     def outward_chunk(ch, carry):
         start = pl.multiple_of(ch * WIDE, WIDE)
-        tiles = pl.ds(pl.multiple_of(4 * ch, 4), 4)
-        wait_bytes(srecv.at[tiles], s_recv.at[ch])
+        quad = pl.ds(pl.multiple_of(4 * ch, 4), 4)
+        wait_bytes(srecv.at[quad], s_recv.at[ch])
         for group in range(2):
             lanes = pl.ds(start + group * LANES, LANES)
             steps = [z8[m : m + 1, lanes] for m in range(MODES)]
@@ -385,7 +389,7 @@
             lanes = slice(group * LANES, (group + 1) * LANES)
             outbuf[rows, lanes] = (longout[rows, lanes] * column).astype(jnp.bfloat16)
 
-    wait_bytes(outgoing, halo_send)
+    wait_bytes(tiles.at[2], halo_send)
     wait_bytes(esend.at[pl.ds(0, seq_count - 1)], e_send)
     wait_bytes(ssend.at[pl.ds(0, seq_count - 1)], s_send)
     wait_bytes(precv.at[others], p_send)
@@ -415,9 +419,7 @@
             vmem(ahead.shape, bf16),
             vmem(pair.shape, bf16),
             vmem(back.shape, bf16),
-            vmem((2, chunks, TILE, WIDE), bf16),
-            vmem((2, chunks, TILE, WIDE), bf16),
-            vmem((chunks, TILE, WIDE), bf16),
+            vmem((3, chunks, TILE, WIDE), bf16),
             vmem((2, chunks, TILE, WIDE), bf16),
             vmem((2, chunks, TILE, WIDE), f32),
             vmem((rows, channels), f32),
@@ -427,6 +429,7 @@
             vmem((chunks, 2 * TILE, WIDE), f32),
             vmem((4, 2 * TILE, WIDE), bf16),
             vmem((2, TILE, WIDE), bf16),
+            vmem((2,) + pair.shape, bf16),
             vmem((2, MODES, channels), f32),
             tiles, tiles, tiles, tiles,
             vmem((rows, LANES), f32),

time: 34.3 us -> 34.3 us (level)
  no operation moved by 1% of the time
where the time goes in v6:
time: 34.3 us; the launch traced here: 34.2 us
  Pallas kernels  33.2 us (97%)
  local copies, waits for them, and re-layouts  0.97 us (3%)
    pallas_call x1, Pallas kernels, on_device(): pl.pallas_call(functools.partial(kernel, seq_count, mp_count), out_shape=...  33.2 us
    unnamed x1, local copies, waits for them, and re-layouts  0.97 us

profile of v6, /device:TPU:1, one launch (start us, length us, event | category | flops | bytes accessed | tf_op | source)
XLA Modules:
  0.0 34.2 jit_solution(6575061001172467458)
XLA Ops:
  0.0 33.2 %shard_map.118 = bf16[256,2048]{1,0:T(8,128)(2,1)S(1)} custom-call(s32[64]{0:T(128)} %docs.1, bf16[256,2048]{1,0:T(8,128)(2,1)} %values_h.1, bf16[256,2048]{1,0:T(8,128)(2,1)} %k1_h.1, bf16[256,2048]{1,0:T(8,128)(2,1)} %q1_h.1, bf16[256,2048]{1,0:T(8,128)(2,1)} %k2_h.1, bf16[256,2048]{1,0:T(8,128)(2,1)} %q2_h.1, bf16[128,2048]{1,0:T(8,128)(2,1)} %taps_h.1, ...), custom_call_target="tpu_custom_call" | custom-call | tf_op jit(solution)/shard_map/pallas_call | solution.py:410
  33.2 1.0 %copy.14 = bf16[256,2048]{1,0:T(8,128)(2,1)} copy(bf16[256,2048]{1,0:T(8,128)(2,1)S(1)} %shard_map.118) | data formatting | bytes 2097152

commit v7 on v6

--- a/solution.py
+++ b/solution.py
@@ -67,17 +67,19 @@
     channels = values.shape[1]
     chunks = channels // WIDE
 
-    def in_copy(source, target, row, ch):
-        cols = pl.ds(ch * WIDE, WIDE)
-        return pltpu.make_async_copy(source.at[:, cols], target.at[:, cols], in_sem.at[row, ch])
+    def in_copies(half, ch):
+        place = (pl.ds(half * TILE, TILE), pl.ds(ch * WIDE, WIDE))
+        return [
+            pltpu.make_async_copy(source.at[place], target.at[place], in_sem.at[2 * half + n, ch])
+            for n, (source, target) in enumerate(((values_h, values), (k1_h, k1)))
+        ]
 
     whole = [(rate_h, rate), (resid_h, resid), (taps_h, taps), (ahead_h, ahead), (pair_h, pair), (back_h, back),
              (q1_h, q1), (k2_h, k2), (q2_h, q2)]
     whole_copies = [pltpu.make_async_copy(a, b, par_sem.at[n]) for n, (a, b) in enumerate(whole)]
-    whole_copies[0].start()
     for ch in range(chunks):
-        in_copy(values_h, values, 0, ch).start()
-        in_copy(k1_h, k1, 1, ch).start()
+        for copy in in_copies(1, ch):
+            copy.start()
 
     barrier = pltpu.get_barrier_semaphore()
 
@@ -89,6 +91,10 @@
     for step in range(1, mp_count):
         pl.semaphore_signal(barrier, inc=1, device_id=(me, lax.rem(part + step, mp_count)), device_id_type=MESH)
 
+    whole_copies[0].start()
+    for ch in range(chunks):
+        for copy in in_copies(0, ch):
+            copy.start()
     for copy in whole_copies[1:]:
         copy.start()
 
@@ -101,6 +107,28 @@
 
     kept0 = flag(jnp.logical_and(me > 0, docs[jnp.maximum(first - 1, 0)] == doc_a))
     kept1 = flag(doc_a == doc_b)
+
+    def gate(half, ch):
+        for copy in in_copies(half, ch):
+            copy.wait()
+        cols = pl.ds(ch * WIDE, WIDE)
+        rows = pl.ds(half * TILE, TILE)
+        product = k1[rows, cols].astype(jnp.float32) * values[rows, cols].astype(jnp.float32)
+        tiles[half + 1, ch] = product.astype(jnp.bfloat16)
+
+    gate(1, 0)
+    pl.semaphore_wait(barrier, seq_count - 1 + mp_count - 1)
+    after = lax.rem(me + 1, seq_count)
+
+    for ch in range(chunks):
+        if ch + 1 < chunks:
+            gate(1, ch + 1)
+        pltpu.make_async_remote_copy(
+            src_ref=tiles.at[2, ch], dst_ref=tiles.at[0, ch], send_sem=halo_send, recv_sem=halo_recv.at[ch],
+            device_id=(after, part), device_id_type=MESH).start()
+
+    for ch in range(chunks):
+        gate(0, ch)
 
     whole_copies[0].wait()
     r_all = rate[...]
@@ -115,28 +143,6 @@
         return carry
 
     lax.fori_loop(0, chunks, fill_zr, 0)
-
-    for ch in range(chunks):
-        in_copy(values_h, values, 0, ch).wait()
-        in_copy(k1_h, k1, 1, ch).wait()
-        cols = pl.ds(ch * WIDE, WIDE)
-        rows = pl.ds(TILE, TILE)
-        product = k1[rows, cols].astype(jnp.float32) * values[rows, cols].astype(jnp.float32)
-        tiles[2, ch] = product.astype(jnp.bfloat16)
-
-    pl.semaphore_wait(barrier, seq_count - 1 + mp_count - 1)
-    after = lax.rem(me + 1, seq_count)
-
-    for ch in range(chunks):
-        pltpu.make_async_remote_copy(
-            src_ref=tiles.at[2, ch], dst_ref=tiles.at[0, ch], send_sem=halo_send, recv_sem=halo_recv.at[ch],
-            device_id=(after, part), device_id_type=MESH).start()
-
-    for ch in range(chunks):
-        cols = pl.ds(ch * WIDE, WIDE)
-        rows = pl.ds(0, TILE)
-        product = k1[rows, cols].astype(jnp.float32) * values[rows, cols].astype(jnp.float32)
-        tiles[1, ch] = product.astype(jnp.bfloat16)
 
     for copy in whole_copies[1:]:
         copy.wait()
@@ -435,7 +441,7 @@
             vmem((rows, LANES), f32),
             vmem((8, LANES), f32),
             vmem((mp_count, 8, LANES), f32),
-            dma((2, chunks)),
+            dma((4, chunks)),
             dma((9,)),
             dma,
             dma((chunks,)),

time: 34.3 us -> 34.2 us (level)
  no operation moved by 1% of the time
where the time goes in v7:
time: 34.2 us; the launch traced here: 34.1 us
  Pallas kernels  33.1 us (97%)
  local copies, waits for them, and re-layouts  0.97 us (3%)
    pallas_call x1, Pallas kernels, on_device(): pl.pallas_call(functools.partial(kernel, seq_count, mp_count), out_shape=...  33.1 us
    unnamed x1, local copies, waits for them, and re-layouts  0.97 us

profile of v7, /device:TPU:1, one launch (start us, length us, event | category | flops | bytes accessed | tf_op | source)
XLA Modules:
  0.0 34.1 jit_solution(2391555634111242084)
XLA Ops:
  0.0 33.1 %shard_map.118 = bf16[256,2048]{1,0:T(8,128)(2,1)S(1)} custom-call(s32[64]{0:T(128)} %docs.1, bf16[256,2048]{1,0:T(8,128)(2,1)} %values_h.1, bf16[256,2048]{1,0:T(8,128)(2,1)} %k1_h.1, bf16[256,2048]{1,0:T(8,128)(2,1)} %q1_h.1, bf16[256,2048]{1,0:T(8,128)(2,1)} %k2_h.1, bf16[256,2048]{1,0:T(8,128)(2,1)} %q2_h.1, bf16[128,2048]{1,0:T(8,128)(2,1)} %taps_h.1, ...), custom_call_target="tpu_custom_call" | custom-call | tf_op jit(solution)/shard_map/pallas_call | solution.py:416
  33.1 1.0 %copy.14 = bf16[256,2048]{1,0:T(8,128)(2,1)} copy(bf16[256,2048]{1,0:T(8,128)(2,1)S(1)} %shard_map.118) | data formatting | bytes 2097152

commit v8 on v7

--- a/solution.py
+++ b/solution.py
@@ -322,7 +322,8 @@
         return (block_decay * through) * state + erecv[n]
 
     def hand_back(step, carry):
-        target = lax.rem(me + step, seq_count)
+        away = 1 + lax.rem(step + seq_count // 2 - 2, seq_count - 1)
+        target = lax.rem(me + away, seq_count)
         pltpu.make_async_remote_copy(
             src_ref=ssend.at[target], dst_ref=srecv.at[me], send_sem=s_send, recv_sem=s_recv.at[slot],
             device_id=(target, part), device_id_type=MESH).start()
@@ -377,7 +378,7 @@
     for half in range(2):
         turned = power[half * TILE : (half + 1) * TILE, :].T
         psend[half : half + 1, :] = jnp.sum(turned, axis=0, keepdims=True)
-    for step in range(1, mp_count):
+    for step in sorted(range(1, mp_count), key=lambda n: abs(n - mp_count // 2)):
         pltpu.make_async_remote_copy(
             src_ref=psend, dst_ref=precv.at[part], send_sem=p_send, recv_sem=p_recv,
             device_id=(me, lax.rem(part + step, mp_count)), device_id_type=MESH).start()

time: 34.2 us -> 34.9 us (1.020)
  Pallas kernels: 33.1 us -> 33.8 us
    pallas_call x1, Pallas kernels: 33.1 us -> 33.8 us  [on_device(): pl.pallas_call(functools.partial(kernel, seq_count, mp_count), out_shape=...]
where the time goes in v8:
time: 34.9 us; the launch traced here: 34.8 us
  Pallas kernels  33.8 us (97%)
  local copies, waits for them, and re-layouts  0.97 us (3%)
    pallas_call x1, Pallas kernels, on_device(): pl.pallas_call(functools.partial(kernel, seq_count, mp_count), out_shape=...  33.8 us
    unnamed x1, local copies, waits for them, and re-layouts  0.97 us

profile of v8, /device:TPU:1, one launch (start us, length us, event | category | flops | bytes accessed | tf_op | source)
XLA Modules:
  0.0 34.8 jit_solution(11931075901183089973)
XLA Ops:
  0.0 33.8 %shard_map.118 = bf16[256,2048]{1,0:T(8,128)(2,1)S(1)} custom-call(s32[64]{0:T(128)} %docs.1, bf16[256,2048]{1,0:T(8,128)(2,1)} %values_h.1, bf16[256,2048]{1,0:T(8,128)(2,1)} %k1_h.1, bf16[256,2048]{1,0:T(8,128)(2,1)} %q1_h.1, bf16[256,2048]{1,0:T(8,128)(2,1)} %k2_h.1, bf16[256,2048]{1,0:T(8,128)(2,1)} %q2_h.1, bf16[128,2048]{1,0:T(8,128)(2,1)} %taps_h.1, ...), custom_call_target="tpu_custom_call" | custom-call | tf_op jit(solution)/shard_map/pallas_call | solution.py:417
  33.8 1.0 %copy.14 = bf16[256,2048]{1,0:T(8,128)(2,1)} copy(bf16[256,2048]{1,0:T(8,128)(2,1)S(1)} %shard_map.118) | data formatting | bytes 2097152
